TPU v7x, 128 devices: a whole 4x4x4 slice. The times are simulated.
128 devices in a mesh: dom: 32 (over z, y_hi, x), rep: 4 (over y_lo, core).
Axes of the slice: x: 4, y: 4 (y_hi: 2, y_lo: 2; y = y_hi * 2 + y_lo), z: 4, core: 2. Of those that a mesh axis runs over, the one named last changes fastest.
Arguments:
- embeddings: float32 [1048576, 256], P(('dom', 'rep')), may hold values from -1.5 to 1.5
- row_state: float32 [1048576], P(('dom', 'rep')), may hold values from 0.01 to 0.1
- relations: float32 [64, 256], replicated, may hold values from 0.1 to 1.9
- rel_state: float32 [64, 256], replicated, may hold values from 2 to 40
- edge_src: int32 [32, 4, 2, 4, 1000], P('dom', 'rep'), may hold values from 0 to 8191
- edge_dst: int32 [32, 4, 2, 4, 1000], P('dom', 'rep'), may hold values from 0 to 8191
- edge_rel: int32 [32, 4, 2, 4, 1000], P('dom', 'rep'), may hold values from 0 to 63
- batch_count: int32 [32, 4, 2], P('dom', 'rep'), may hold values from 1 to 4, as said below
Outputs:
- new_embeddings: float32 [1048576, 256], P(('dom', 'rep'))
- new_row_state: float32 [1048576], P(('dom', 'rep'))
- new_relations: float32 [64, 256], replicated
- new_rel_state: float32 [64, 256], replicated
Inputs may be any that keep to these rules, and one draw needn't show every extreme that they name: `batch_count`: batches at or past the count are ignored; some bucket of each round set reaches 4.
All inputs are finite; a program needn't handle non-finite values.
Results may differ from a plain program's by a relative error of at most 0.0031.
Values may be sent and summed in bfloat16 or wider, within the bound.
A program may use at most 128 MiB of HBM per device.

v0:
```python
import functools

import jax
import jax.numpy as jnp
from jax import lax
from jax.experimental import pallas as pl
from jax.experimental.pallas import tpu as pltpu
from jax.sharding import PartitionSpec as P


ROUNDS = 2

learn_rate = 0.1
rel_rate = 0.1


SMEM = pl.BlockSpec(memory_space=pltpu.SMEM)
VMEM = pl.BlockSpec(memory_space=pltpu.VMEM)
ANY = pl.BlockSpec(memory_space=pl.ANY)
HBM = pl.BlockSpec(memory_space=pltpu.HBM)
GATHER_UNROLL = 20
SCATTER_UNROLL = 8
BLOCK = 256
LANES = 128
MIB = 1024 * 1024


def params(mib, **kw):
    return pltpu.CompilerParams(vmem_limit_bytes=mib * MIB, **kw)


def cost(nbytes):
    return pl.CostEstimate(flops=0, bytes_accessed=nbytes, transcendentals=0)


def round_up(n, m):
    return (n + m - 1) // m * m


def piece(row):
    return pl.ds(pl.multiple_of(row * 2, 2), 2)


def half(start, count, side):
    return pl.ds(start * 2 + side, count, stride=2)


def gather_rows(index_ref, batches, count, table, rows, out):
    height = rows.shape[0] // 2
    if height > count:
        rows[2 * count :, :] = jnp.zeros((2 * (height - count), LANES), rows.dtype)
    for place, batch in enumerate(batches):

        @pl.loop(0, count // GATHER_UNROLL)
        def _(step):
            base = step * GATHER_UNROLL
            for j in range(GATHER_UNROLL):
                rows[piece(base + j), :] = table[piece(index_ref[batch * count + base + j]), :]

        for side in range(2):
            out[place * height : (place + 1) * height, side * LANES : (side + 1) * LANES] = rows[
                half(0, height, side), :
            ].astype(out.dtype)


def scatter_rows(jobs, count):
    @pl.loop(0, count // SCATTER_UNROLL)
    def _(step):
        base = step * SCATTER_UNROLL
        for j in range(SCATTER_UNROLL):
            spots = [piece(job[0][job[1] * count + base + j]) for job in jobs]
            olds = [job[4][spot, :] for spot, job in zip(spots, jobs)]
            for spot, old, (_, _, rows, start, total) in zip(spots, olds, jobs):
                total[spot, :] = old + rows[piece(start + base + j), :]


def scatter_live(live_ref, jobs, count):
    for first in range(0, len(jobs), 2):
        pair = jobs[first : first + 2]
        if len(pair) == 2:

            @pl.when(pair[1][1] < live_ref[0])
            def _():
                scatter_rows(pair, count)

        @pl.when((pair[0][1] < live_ref[0]) & (pair[-1][1] >= live_ref[0]))
        def _():
            scatter_rows(pair[:1], count)


def jobs_of(index, first, group_rows, totals, groups):
    jobs = []
    for group, rows in zip(groups[first:], group_rows):
        height = rows.shape[0] // (2 * len(group))
        for place, batch in enumerate(group):
            jobs.append((index, batch, rows, place * height, totals[batch % 2]))
    return jobs


def spread(ref, rows):
    for side in range(2):
        rows[half(0, ref.shape[0], side), :] = ref[:, side * LANES : (side + 1) * LANES].astype(
            jnp.float32
        )


def pack_first(index, table, edge_dst, edge_rel, batch_count, batches):
    rounds, slots, count = edge_dst.shape
    height = round_up(count, 16)
    row_count, width = table.shape
    parts = 8
    part_rows = row_count // parts

    def body(index_ref, count_ref, table_hbm, dst_ref, rel_ref, long_hbm, *refs):
        notes, refs = refs[:rounds], refs[rounds:]
        out, table_v, long_v, rows, sems = refs
        loads = []
        for part in range(parts):
            here = pl.ds(part * part_rows, part_rows)
            load = pltpu.make_async_copy(table_hbm.at[here], table_v.at[here], sems.at[part])
            load.start()
            loads.append(load)
        for number, note in enumerate(notes):
            note[:slots] = dst_ref[number]
            note[slots : 2 * slots] = rel_ref[number]
            note[2 * slots :] = jnp.full((1, count), count_ref[number], jnp.int32)
        for part in range(parts):
            loads[part].wait()

            @pl.loop(part * part_rows // LANES, (part + 1) * part_rows // LANES)
            def _(step):
                here = pl.multiple_of(step * LANES, LANES)
                for side in range(2):
                    long_v[half(here, LANES, side), :] = table_v[
                        pl.ds(here, LANES), side * LANES : (side + 1) * LANES
                    ]

        save = pltpu.make_async_copy(long_v, long_hbm, sems.at[parts])
        save.start()
        gather_rows(index_ref, batches, count, long_v, rows, out)
        save.wait()

    return pl.pallas_call(
        body,
        out_shape=[jax.ShapeDtypeStruct((2 * row_count, LANES), jnp.float32)]
        + [jax.ShapeDtypeStruct((2 * slots + 1, count), jnp.int32)] * rounds
        + [jax.ShapeDtypeStruct((len(batches) * height, width), jnp.bfloat16)],
        in_specs=[SMEM, SMEM, HBM, VMEM, VMEM],
        out_specs=[HBM] + [VMEM] * (rounds + 1),
        scratch_shapes=[
            pltpu.VMEM((row_count, width), jnp.float32),
            pltpu.VMEM((2 * row_count, LANES), jnp.float32),
            pltpu.VMEM((2 * height, LANES), jnp.float32),
            pltpu.SemaphoreType.DMA((parts + 1,)),
        ],
        compiler_params=params(56),
        cost_estimate=cost(25_000_000),
        name="pack_first",
    )(index, batch_count, table, edge_dst, edge_rel)


def pack(index, table, groups, count, width, grant):
    height = round_up(count, 16)

    def body(index_ref, table_hbm, *refs):
        outs, (table_v, rows, sem) = refs[:-3], refs[-3:]
        load = pltpu.make_async_copy(table_hbm, table_v, sem)
        load.start()
        load.wait()
        for out, group in zip(outs, groups):
            gather_rows(index_ref, group, count, table_v, rows, out)

    return pl.pallas_call(
        body,
        out_shape=[
            jax.ShapeDtypeStruct((len(group) * height, width), jnp.bfloat16) for group in groups
        ],
        in_specs=[SMEM, HBM],
        out_specs=[VMEM] * len(groups),
        scratch_shapes=[
            pltpu.VMEM(table.shape, jnp.float32),
            pltpu.VMEM((2 * height, LANES), jnp.float32),
            pltpu.SemaphoreType.DMA,
        ],
        compiler_params=params(grant),
        cost_estimate=cost(30_000_000),
    )(index, table)


def batch_kernel(group, count, live_ref, kind_ref, source_ref, target_ref, rel_ref, rel_in,
                 grad_source, grad_target, rel_out, query_t, total_t, product):
    height, width = source_ref.shape[0] // len(group), source_ref.shape[1]
    full = round_up(height, BLOCK)
    kinds = rel_ref.shape[0]
    neg_share = 0.5 / (count - 1)
    rel_out[...] = rel_in[...]

    @pl.loop(0, jnp.clip(live_ref[0] - group[0], 0, len(group)))
    def _(place):
        start = pl.multiple_of(place * height, 16)
        rel = rel_ref[...]
        high = rel.astype(jnp.bfloat16)
        rest = rel - high.astype(jnp.float32)
        mid = rest.astype(jnp.bfloat16)
        low = (rest - mid.astype(jnp.float32)).astype(jnp.bfloat16)
        parts = jnp.concatenate([high, mid, low], axis=0)
        kind = jnp.broadcast_to(kind_ref[pl.ds(place, 1), :], (3 * kinds, full))
        row = lax.broadcasted_iota(jnp.int32, (3 * kinds, full), 0)
        hot = jnp.where((row % kinds) == kind, 1.0, 0.0).astype(jnp.bfloat16)
        diagonal = lax.dot_general(
            hot, parts, (((0,), (0,)), ((), ())), preferred_element_type=jnp.float32
        )
        source = source_ref[pl.ds(start, height), :].astype(jnp.float32)
        target = target_ref[pl.ds(start, height), :]
        if full > height:
            gap = jnp.zeros((full - height, width), jnp.float32)
            source = jnp.concatenate([source, gap], axis=0)
            target = jnp.concatenate([target, gap.astype(target.dtype)], axis=0)
        query_full = (source * diagonal).astype(jnp.bfloat16).astype(jnp.float32)
        query_t[...] = query_full.T.astype(jnp.bfloat16)
        half_query = (query_full * 0.5).astype(jnp.bfloat16)
        eye = lax.broadcasted_iota(jnp.int32, (BLOCK, BLOCK), 0) == lax.broadcasted_iota(
            jnp.int32, (BLOCK, BLOCK), 1
        )
        for block in range(full // BLOCK):
            here = slice(block * BLOCK, (block + 1) * BLOCK)
            pieces = []
            for col in range(full // BLOCK):
                there = slice(col * BLOCK, (col + 1) * BLOCK)
                slope = jnp.tanh(
                    lax.dot_general(
                        half_query[here],
                        target[there],
                        (((1,), (1,)), ((), ())),
                        preferred_element_type=jnp.float32,
                    )
                )
                weight = slope * neg_share + neg_share
                if col == block:
                    weight = jnp.where(eye, slope * 0.5 - 0.5, weight)
                pieces.append(weight.astype(jnp.bfloat16))
            weights = jnp.concatenate(pieces, axis=1)
            grad_query = jnp.dot(weights, target, preferred_element_type=jnp.float32)
            tall = min(height - block * BLOCK, BLOCK)
            grad_rows = (grad_query * diagonal[here])[:tall]
            spot = pl.multiple_of(start + block * BLOCK, 16)
            grad_source[pl.ds(spot, tall), :] = grad_rows.astype(grad_source.dtype)
            product[here, :] = grad_query * source[here]
            part = jnp.dot(query_t[:, here], weights, preferred_element_type=jnp.float32)
            if block == 0:
                total_t[...] = part
            else:
                total_t[...] += part
        grad_rows = total_t[...].T[:height]
        for side in range(2):
            grad_target[half(start, height, side), :] = grad_rows[:, side * LANES : (side + 1) * LANES]
        value = product[...]
        upper = value.astype(jnp.bfloat16)
        lower = (value - upper.astype(jnp.float32)).astype(jnp.bfloat16)
        one = hot[:kinds]
        rel_out[...] = (
            rel_out[...]
            + jnp.dot(one, upper, preferred_element_type=jnp.float32)
            + jnp.dot(one, lower, preferred_element_type=jnp.float32)
        )


def run_group(group, count, live, kind, source, target, relations, rel_grad):
    height, width = source.shape
    full = round_up(height // len(group), BLOCK)
    return pl.pallas_call(
        functools.partial(batch_kernel, group, count),
        out_shape=[
            jax.ShapeDtypeStruct((height, width), jnp.bfloat16),
            jax.ShapeDtypeStruct((2 * height, LANES), jnp.float32),
            jax.ShapeDtypeStruct(rel_grad.shape, jnp.float32),
        ],
        in_specs=[SMEM] + [VMEM] * 5,
        out_specs=[VMEM] * 3,
        scratch_shapes=[
            pltpu.VMEM((width, full), jnp.bfloat16),
            pltpu.VMEM((width, full), jnp.float32),
            pltpu.VMEM((full, width), jnp.float32),
        ],
        compiler_params=params(24),
        cost_estimate=cost(15_000_000),
        name="batch_terms",
    )(live, kind, source, target, relations, rel_grad)


def first_total(count, groups, row_count, live, other_live, source_index, other_index, own, returned):
    def body(live_ref, other_ref, source_ref, index_ref, *refs):
        own_refs = refs[: len(own)]
        back_refs = refs[len(own) : len(own) + len(returned)]
        total, other = refs[len(own) + len(returned) :][:2]
        rows = refs[len(own) + len(returned) + 2 :]
        totals = (total, other)
        total[...] = jnp.zeros_like(total)
        other[...] = jnp.zeros_like(other)
        for ref, long in zip(back_refs, rows):
            spread(ref, long)
        scatter_live(
            live_ref,
            jobs_of(source_ref, 0, own_refs, totals, groups),
            count,
        )
        scatter_live(
            other_ref,
            jobs_of(index_ref, 0, rows, totals, groups),
            count,
        )
        total[...] += other[...]

    return pl.pallas_call(
        body,
        out_shape=jax.ShapeDtypeStruct((2 * row_count, LANES), jnp.float32),
        in_specs=[SMEM] * 4 + [VMEM] * (len(own) + len(returned)),
        out_specs=VMEM,
        scratch_shapes=[pltpu.VMEM((2 * row_count, LANES), jnp.float32)]
        + [pltpu.VMEM(own[0].shape, jnp.float32)] * len(returned),
        compiler_params=params(50),
        cost_estimate=cost(60_000_000),
        name="first_total",
    )(live, other_live, source_index, other_index, *own, *returned)


def finish(
    count, groups, live, source_index, total, returned, first, table, state, width, near, relations, rel_state, next_index, next_batches
):
    row_count = table.shape[0] // 2
    height = returned[0].shape[0]
    tiles = row_count // LANES
    step_rows = 1024
    steps = row_count // step_rows
    last = next_index is None
    indices = [live, source_index] + ([] if last else [next_index])

    def body(*refs):
        refs = list(refs)

        def take(number):
            taken = refs[:number]
            del refs[:number]
            return taken

        live_ref, index_ref, *next_ref = take(len(indices))
        (total_hbm,) = take(1)
        back_refs = take(len(returned))
        table_hbm, state_ref = take(2)
        near_refs = take(len(near))
        rel_ref, rel_state_ref, out_hbm, state_out, new_rel, new_rel_state = take(6)
        next_outs = take(0 if last else 1)
        total_v, other_v, table_v, state_t, mean_t, sems = take(6)
        rows = take(len(returned))
        out_v = refs[0] if last else table_v
        load_total = pltpu.make_async_copy(total_hbm, total_v, sems.at[0])
        load_table = pltpu.make_async_copy(table_hbm, table_v, sems.at[1])
        load_total.start()
        load_table.start()
        other_v[...] = jnp.zeros_like(other_v)
        for ref, long in zip(back_refs, rows):
            spread(ref, long)
        rel_total = pair_sum([ref[...] for ref in near_refs])
        rel_new = rel_state_ref[...] + rel_total * rel_total
        new_rel_state[...] = rel_new
        new_rel[...] = rel_ref[...] - rel_rate * rel_total / jnp.sqrt(rel_new)
        spare = jnp.zeros((LANES - tiles, LANES), jnp.float32)
        state_t[...] = jnp.concatenate([state_ref[...], spare], axis=0).T
        mean_t[...] = jnp.zeros_like(mean_t)
        load_total.wait()
        totals = (other_v, total_v)
        scatter_live(
            live_ref,
            jobs_of(index_ref, first, rows, totals, groups),
            count,
        )
        load_table.wait()
        lane = lax.broadcasted_iota(jnp.int32, (LANES, LANES), 1)
        saves = []
        for step in range(steps):

            @pl.loop(step * step_rows // LANES, (step + 1) * step_rows // LANES)
            def _(group):
                base = pl.multiple_of(group * LANES, LANES)
                sides = [half(base, LANES, side) for side in range(2)]
                grads = [total_v[side, :] + other_v[side, :] for side in sides]
                square = grads[0] * grads[0] + grads[1] * grads[1]
                mean = jnp.sum(square, axis=1, keepdims=True) * (1.0 / width)
                mine = lane == group
                old = jnp.sum(jnp.where(mine, state_t[...], 0.0), axis=1, keepdims=True)
                mean_t[...] = jnp.where(mine, mean, mean_t[...])
                scale = learn_rate / jnp.sqrt(old + mean)
                values = [table_v[side, :] - grad * scale for side, grad in zip(sides, grads)]
                for number, value in enumerate(values):
                    if last:
                        out_v[pl.ds(base, LANES), number * LANES : (number + 1) * LANES] = value
                    else:
                        out_v[sides[number], :] = value

            tall = step_rows if last else 2 * step_rows
            part = pl.ds(step * tall, tall)
            save = pltpu.make_async_copy(out_v.at[part], out_hbm.at[part], sems.at[2 + step])
            save.start()
            saves.append(save)
        state_out[...] = (state_t[...] + mean_t[...]).T[:tiles]
        for out in next_outs:
            gather_rows(
                next_ref[0], next_batches, count, table_v, rows[0].at[: 2 * round_up(count, 16)], out
            )
        for save in saves:
            save.wait()

    out_shape = (row_count, width) if last else table.shape
    rel_shape = jax.ShapeDtypeStruct(relations.shape, jnp.float32)
    return pl.pallas_call(
        body,
        out_shape=[
            jax.ShapeDtypeStruct(out_shape, jnp.float32),
            jax.ShapeDtypeStruct((tiles, LANES), jnp.float32),
            rel_shape,
            rel_shape,
        ]
        + [jax.ShapeDtypeStruct((len(next_batches) * round_up(count, 16), width), jnp.bfloat16)]
        * (not last),
        in_specs=[SMEM] * len(indices)
        + [ANY]
        + [VMEM] * len(returned)
        + [HBM]
        + [VMEM] * (len(near) + 3),
        out_specs=[HBM] + [VMEM] * (3 + (not last)),
        scratch_shapes=[
            pltpu.VMEM(table.shape, jnp.float32),
            pltpu.VMEM(table.shape, jnp.float32),
            pltpu.VMEM(table.shape, jnp.float32),
            pltpu.VMEM((LANES, LANES), jnp.float32),
            pltpu.VMEM((LANES, LANES), jnp.float32),
            pltpu.SemaphoreType.DMA((2 + steps,)),
        ]
        + [pltpu.VMEM((2 * height, LANES), jnp.float32)] * len(returned)
        + ([pltpu.VMEM((row_count, width), jnp.float32)] if last else []),
        compiler_params=params(50),
        cost_estimate=cost(50_000_000),
        name="finish_last" if last else "finish_next",
    )(*indices, total, *returned, table, state, *near, relations, rel_state)


def flip(index, bits):
    for place in range(8):
        step = 1 << place
        if bits & step:
            index = index + step * (1 - 2 * ((index // step) % 2))
    return index


def relation_kernel(stages, own, summed, *scratch):
    parts, received = (own,) + scratch[:-3], scratch[-3]
    send_sems, recv_sems = scratch[-2:]
    dom, rep = lax.axis_index("dom"), lax.axis_index("rep")

    def device(peer):
        return (flip(dom, peer[0]), flip(rep, peer[1]))

    barrier = pltpu.get_barrier_semaphore()
    peers = [peer for stage in stages for peer in stage]
    for peer in peers:
        pl.semaphore_signal(
            barrier, inc=1, device_id=device(peer), device_id_type=pl.DeviceIdType.MESH
        )
    pl.semaphore_wait(barrier, len(peers))
    slot = 0
    for number, stage in enumerate(stages):
        copies = []
        for peer in stage:
            copy = pltpu.make_async_remote_copy(
                src_ref=parts[number],
                dst_ref=received.at[slot],
                send_sem=send_sems.at[slot],
                recv_sem=recv_sems.at[slot],
                device_id=device(peer),
                device_id_type=pl.DeviceIdType.MESH,
            )
            copy.start()
            copies.append(copy)
            slot += 1
        for copy in copies:
            copy.wait()
        first = slot - len(stage)
        total = pair_sum([parts[number][...]] + [received[first + i] for i in range(len(stage))])
        if number + 1 < len(stages):
            parts[number + 1][...] = total
    summed[...] = total


def pair_sum(values):
    while len(values) > 1:
        values = [values[i] + values[i + 1] for i in range(0, len(values), 2)]
    return values[0]


def relation_sum(rel_grad):
    stages = [
        [(0, 1), (0, 2), (0, 3)],
        [(1, 0), (2, 0), (3, 0)],
        [(4, 0)],
    ]
    slots = sum(len(stage) for stage in stages)
    shape = rel_grad.shape
    return pl.pallas_call(
        functools.partial(relation_kernel, stages),
        out_shape=jax.ShapeDtypeStruct(shape, jnp.float32),
        in_specs=[VMEM],
        out_specs=VMEM,
        scratch_shapes=[pltpu.VMEM(shape, jnp.float32)] * (len(stages) - 1)
        + [
            pltpu.VMEM((slots,) + shape, jnp.float32),
            pltpu.SemaphoreType.DMA((slots,)),
            pltpu.SemaphoreType.DMA((slots,)),
        ],
        compiler_params=pltpu.CompilerParams(
            collective_id=0, has_side_effects=True, vmem_limit_bytes=4 * MIB
        ),
        cost_estimate=cost(20_000_000),
        name="relation_sum",
    )(rel_grad)


def from_partner(shard, axis, distance):
    return from_peer(shard, axis, 1 << distance)


def from_peer(shard, axis, bits):
    return lax.ppermute(shard, axis, [(i, i ^ bits) for i in range(lax.axis_size(axis))])


def on_device(
    embeddings, row_state, relations, rel_state, edge_src, edge_dst, edge_rel, batch_count
):
    bit_count = lax.axis_size("dom").bit_length() - 1
    row_count, width = embeddings.shape
    batches, count = edge_src.shape[-2:]
    padded = round_up(count, BLOCK)
    state = row_state.reshape(row_count // LANES, LANES)
    spots = [bit_count - 1 - number for number in range(ROUNDS)]
    groups = tuple(
        tuple(range(first, min(first + 2, batches))) for first in range(0, batches, 2)
    )
    sources = [edge_src[0, 0, number].reshape(-1) for number in range(ROUNDS)]
    table, *told = pack_first(
        sources[0], embeddings, edge_dst[0, 0], edge_rel[0, 0], batch_count[0, 0], groups[0]
    )
    told, sent = told[:ROUNDS], told[ROUNDS:]
    for number in range(ROUNDS):
        last = number + 1 == ROUNDS
        swap_bit = spots[number]
        source_index = sources[number]
        live = batch_count[0, 0, number].reshape(1)
        note = from_partner(told[number], "dom", swap_bit)
        arrived = [from_partner(sent[0], "dom", swap_bit)]
        more = pack(source_index, table, groups[1:], count, width, 54)
        for rows in more:
            arrived.append(from_partner(rows, "dom", swap_bit))
        other_index = note[:batches].reshape(-1)
        other_live = note[2 * batches, :1]
        kinds = jnp.pad(
            note[batches : 2 * batches], ((0, 0), (0, padded - count)), constant_values=-1
        )
        targets = pack(other_index, table, groups, count, width, 50)
        rel_grad = jnp.zeros(relations.shape, jnp.float32)
        own, returned = [], []
        for place, group in enumerate(groups):
            grad_source, grad_target, rel_grad = run_group(
                group,
                count,
                other_live,
                kinds[group[0] : group[-1] + 1],
                arrived[place],
                targets[place],
                relations,
                rel_grad,
            )
            own.append(grad_target)
            returned.append(from_partner(grad_source, "dom", swap_bit))
        near = [relation_sum(rel_grad)]
        for bits in (8, 16, 24):
            near.append(from_peer(near[0], "dom", bits))
        early = len(groups) - 1
        total = first_total(
            count, groups, row_count, other_live, live, other_index, source_index, own, returned[:early]
        )
        table, state, relations, rel_state, *sent = finish(
            count,
            groups,
            live,
            source_index,
            total,
            returned[early:],
            early,
            table,
            state,
            width,
            near,
            relations,
            rel_state,
            None if last else sources[number + 1],
            () if last else groups[0],
        )
    return (table, state.reshape(row_count), relations, rel_state)


def solution(mesh):
    return sharded(mesh)


def sharded(mesh):
    return jax.shard_map(
        on_device,
        mesh=mesh,
        in_specs=(
            P(("dom", "rep"), None),
            P(("dom", "rep")),
            P(),
            P(),
            P("dom", "rep", None, None, None),
            P("dom", "rep", None, None, None),
            P("dom", "rep", None, None, None),
            P("dom", "rep", None),
        ),
        out_specs=(P(("dom", "rep"), None), P(("dom", "rep")), P(), P()),
        check_vma=False,
    )
```

profile of v0, /device:TPU:4, one launch (start us, length us, event | category | flops | bytes accessed | tf_op | source)
XLA Modules:
  0.0 285.9 jit_solution(17371795067043625789)
XLA Ops:
  0.6 0.7 fusion.2
  1.4 0.7 reshape_squeeze.14.index_ref.refs_1_
  2.1 8.9 %pack_first.1 = (f32[16384,128]{1,0:T(8,128)}, s32[9,1000]{1,0:T(8,128)}, s32[9,1000]{1,0:T(8,128)}, bf16[2016,256]{1,0:T(8,128)(2,1)}) custom-call(s32[4000]{0:T(1024)} %reshape_squeeze.14.index_ref.refs_1_, s32[2]{0:T(128)} %bitcast.12, f32[8192,256]{1,0:T(8,128)} %table_hbm.1, s32[2,4,1000]{2,1,0:T(4,128)} %bitcast.10, s32[2,4,1000]{2,1,0:T(4,128)} %bitcast.11), custom_call_target="tpu_custom_call" | custom-call | bytes 25000000 | tf_op jit(solution)/shard_map/pack_first/pallas_call | solution.py:143
  11.0 0.0 copy-start.12
  11.0 4.0 %collective-permute-start.2 = (bf16[2016,256]{1,0:T(8,128)(2,1)}, bf16[2016,256]{1,0:T(8,128)(2,1)S(1)}, u32[]{:S(2)}, u32[]{:S(2)}) collective-permute-start(bf16[2016,256]{1,0:T(8,128)(2,1)} %get-tuple-element.35), channel_id=1, source_target_pairs={{0,64},{4,68},{8,72},{12,76},{16,80},{20,84},{24,88},{28,92},{32,9... | collective-permute-start | bytes 3096584 | tf_op jit(solution)/shard_map/ppermute | solution.py:532
  15.0 8.3 %shard_map.112 = bf16[2016,256]{1,0:T(8,128)(2,1)} custom-call(s32[4000]{0:T(1024)} %reshape_squeeze.14.index_ref.refs_1_, f32[16384,128]{1,0:T(8,128)} %get-tuple-element.36.table_hbm.refs_5_), custom_call_target="tpu_custom_call" | custom-call | bytes 30000000 | tf_op jit(solution)/shard_map/pallas_call | solution.py:173
  23.2 0.0 copy-start.10
  23.3 0.1 collective-permute-start.3
  23.4 3.5 %collective-permute-start.1 = (s32[9,1000]{1,0:T(8,128)S(1)}, s32[9,1000]{1,0:T(8,128)S(1)}, u32[]{:S(2)}, u32[]{:S(2)}) collective-permute-start(s32[9,1000]{1,0:T(8,128)S(1)} %copy-done.12), channel_id=1, source_target_pairs={{0,64},{4,68},{8,72},{12,76},{16,80},{20,84},{24,88},{28,92},{32,9... | collective-permute-start | bytes 108008 | tf_op jit(solution)/shard_map/ppermute | solution.py:532
  26.9 34.6 %collective-permute-done.1 = s32[9,1000]{1,0:T(8,128)S(1)} collective-permute-done((s32[9,1000]{1,0:T(8,128)S(1)}, s32[9,1000]{1,0:T(8,128)S(1)}, u32[]{:S(2)}, u32[]{:S(2)}) %collective-permute-start.1) | collective-permute-done | bytes 36032 | tf_op jit(solution)/shard_map/ppermute | solution.py:532
  61.5 0.1 reshape.21.index_ref.source_ref
  61.6 9.7 %shard_map.111 = (bf16[2016,256]{1,0:T(8,128)(2,1)S(1)}, bf16[2016,256]{1,0:T(8,128)(2,1)S(1)}) custom-call(s32[4000]{0:T(1024)S(1)} %reshape.21.index_ref.source_ref, f32[16384,128]{1,0:T(8,128)} %get-tuple-element.36.table_hbm.refs_5_), custom_call_target="tpu_custom_call" | custom-call | bytes 30000000 | tf_op jit(solution)/shard_map/pallas_call | solution.py:173
  71.3 0.5 slice.59
  71.9 1.0 copy-done.2
  72.8 1.2 copy-done.3
  74.0 6.4 %batch_terms.4 = (bf16[2016,256]{1,0:T(8,128)(2,1)}, f32[4032,128]{1,0:T(8,128)S(1)}, f32[64,256]{1,0:T(8,128)S(1)}) custom-call(s32[1]{0:T(128)} %bitcast.6.live_ref, s32[2,1024]{1,0:T(2,128)S(1)} %get-tuple-element.71.kind_ref, bf16[2016,256]{1,0:T(8,128)(2,1)S(1)} %copy-done.3, bf16[2016,256]{1,0:T(8,128)(2,1)S(1)} %get-tuple-element.37.target_ref, ...), custom_call_target="tpu_custom_call" | custom-call | bytes 15000000 | tf_op jit(solution)/shard_map/batch_terms/pallas_call | solution.py:271
  80.4 0.8 collective-permute-start.4
  81.2 1.5 batch_terms.5
  82.8 1.4 copy-done
  84.1 2.7 collective-permute-start.5
  86.8 0.1 reshape_squeeze.13.refs_2_.index_ref.refs_1_
  86.9 20.4 %relation_sum.2.refs_7_ = f32[64,256]{1,0:T(8,128)S(1)} custom-call(f32[64,256]{1,0:T(8,128)S(1)} %get-tuple-element.44.own), custom_call_target="tpu_custom_call" | custom-call | bytes 20000000 | tf_op jit(solution)/shard_map/relation_sum/pallas_call | solution.py:508
  107.4 0.4 collective-permute-start.8
  107.7 1.3 collective-permute-start.7
  109.0 2.5 collective-permute-start.6
  111.5 0.7 fusion.3
  112.2 15.6 %first_total.2.refs_3_ = f32[16384,128]{1,0:T(8,128)} custom-call(s32[1]{0:T(128)} %bitcast.6.live_ref, s32[1]{0:T(128)} %bitcast.5.other_ref.refs_0_, s32[4000]{0:T(1024)S(1)} %reshape.21.index_ref.source_ref, s32[4000]{0:T(1024)S(1)} %copy-done.5, f32[4032,128]{1,0:T(8,128)S(1)} %get-tuple-element.38.refs_0_, f32[4032,128]{1,0:T(8,128)} %copy-done, ...), custom_call_target="tpu_custom_call" | custom-call | bytes 60000000 | tf_op jit(solution)/shard_map/first_total/pallas_call | solution.py:314
  127.8 2.7 collective-permute-done.8.refs_10_
  130.5 1.0 collective-permute-done.6.refs_8_
  131.6 20.4 %finish_next.1 = (f32[16384,128]{1,0:T(8,128)}, f32[64,128]{1,0:T(8,128)S(1)}, f32[64,256]{1,0:T(8,128)S(1)}, f32[64,256]{1,0:T(8,128)S(1)}, bf16[2016,256]{1,0:T(8,128)(2,1)}) custom-call(s32[1]{0:T(128)} %bitcast.5.other_ref.refs_0_, s32[4000]{0:T(1024)S(1)} %copy-done.5, s32[4000]{0:T(1024)S(1)} %reshape_squeeze.13.refs_2_.index_ref.refs_1_, ...), custom_call_target="tpu_custom_call" | custom-call | bytes 50000000 | tf_op jit(solution)/shard_map/finish_next/pallas_call | solution.py:415
  151.9 3.8 %collective-permute-start.9 = (bf16[2016,256]{1,0:T(8,128)(2,1)}, bf16[2016,256]{1,0:T(8,128)(2,1)S(1)}, u32[]{:S(2)}, u32[]{:S(2)}) collective-permute-start(bf16[2016,256]{1,0:T(8,128)(2,1)} %get-tuple-element.45), channel_id=1, source_target_pairs={{0,32},{4,36},{8,40},{12,44},{16,48},{20,52},{24,56},{28,60},{32,0... | collective-permute-start | bytes 3096584 | tf_op jit(solution)/shard_map/ppermute | solution.py:532
  155.8 8.1 %shard_map.114 = bf16[2016,256]{1,0:T(8,128)(2,1)} custom-call(s32[4000]{0:T(1024)} %copy-done.6, f32[16384,128]{1,0:T(8,128)} %get-tuple-element.46.table_hbm.refs_4_), custom_call_target="tpu_custom_call" | custom-call | bytes 30000000 | tf_op jit(solution)/shard_map/pallas_call | solution.py:173
  163.9 0.1 collective-permute-start.10
  164.0 2.0 collective-permute-start
  166.0 33.8 %collective-permute-done = s32[9,1000]{1,0:T(8,128)S(1)} collective-permute-done((s32[9,1000]{1,0:T(8,128)S(1)}, s32[9,1000]{1,0:T(8,128)S(1)}, u32[]{:S(2)}, u32[]{:S(2)}) %collective-permute-start) | collective-permute-done | bytes 36032 | tf_op jit(solution)/shard_map/ppermute | solution.py:532
  199.8 0.1 reshape.20.index_ref.source_ref
  199.9 0.5 slice.56
  200.4 9.7 %shard_map.113 = (bf16[2016,256]{1,0:T(8,128)(2,1)S(1)}, bf16[2016,256]{1,0:T(8,128)(2,1)S(1)}) custom-call(s32[4000]{0:T(1024)S(1)} %reshape.20.index_ref.source_ref, f32[16384,128]{1,0:T(8,128)} %get-tuple-element.46.table_hbm.refs_4_), custom_call_target="tpu_custom_call" | custom-call | bytes 30000000 | tf_op jit(solution)/shard_map/pallas_call | solution.py:173
  210.2 5.5 %batch_terms.6 = (bf16[2016,256]{1,0:T(8,128)(2,1)S(1)}, f32[4032,128]{1,0:T(8,128)S(1)}, f32[64,256]{1,0:T(8,128)S(1)}) custom-call(s32[1]{0:T(128)} %bitcast.4.live_ref, s32[2,1024]{1,0:T(2,128)S(1)} %get-tuple-element.69.kind_ref, bf16[2016,256]{1,0:T(8,128)(2,1)S(1)} %collective-permute-done.9.source_ref, ...), custom_call_target="tpu_custom_call" | custom-call | bytes 15000000 | tf_op jit(solution)/shard_map/batch_terms/pallas_call | solution.py:271
  215.7 1.8 collective-permute-start.11
  217.5 5.5 %batch_terms.7 = (bf16[2016,256]{1,0:T(8,128)(2,1)S(1)}, f32[4032,128]{1,0:T(8,128)S(1)}, f32[64,256]{1,0:T(8,128)S(1)}) custom-call(s32[1]{0:T(128)} %bitcast.4.live_ref, s32[2,1024]{1,0:T(2,128)S(1)} %get-tuple-element.68.kind_ref, bf16[2016,256]{1,0:T(8,128)(2,1)S(1)} %collective-permute-done.10.source_ref, ...), custom_call_target="tpu_custom_call" | custom-call | bytes 15000000 | tf_op jit(solution)/shard_map/batch_terms/pallas_call | solution.py:271
  223.0 1.3 copy-done.1
  224.3 17.4 %relation_sum.3.refs_6_ = f32[64,256]{1,0:T(8,128)S(1)} custom-call(f32[64,256]{1,0:T(8,128)S(1)} %get-tuple-element.56.own), custom_call_target="tpu_custom_call" | custom-call | bytes 20000000 | tf_op jit(solution)/shard_map/relation_sum/pallas_call | solution.py:508
  241.8 2.0 collective-permute-start.15
  243.8 1.6 collective-permute-start.14
  245.3 0.6 collective-permute-start.13
  245.9 21.2 %first_total.3.refs_2_ = f32[16384,128]{1,0:T(8,128)} custom-call(s32[1]{0:T(128)} %bitcast.4.live_ref, s32[1]{0:T(128)} %bitcast.other_ref.refs_0_, s32[4000]{0:T(1024)S(1)} %reshape.20.index_ref.source_ref, s32[4000]{0:T(1024)S(1)} %copy-done.7, f32[4032,128]{1,0:T(8,128)S(1)} %get-tuple-element.49.refs_0_, f32[4032,128]{1,0:T(8,128)} %copy-done.1, ...), custom_call_target="tpu_custom_call" | custom-call | bytes 60000000 | tf_op jit(solution)/shard_map/first_total/pallas_call | solution.py:314
  267.1 18.6 %finish_last.1 = (f32[8192,256]{1,0:T(8,128)}, f32[64,128]{1,0:T(8,128)}, f32[64,256]{1,0:T(8,128)}, f32[64,256]{1,0:T(8,128)}) custom-call(s32[1]{0:T(128)} %bitcast.other_ref.refs_0_, s32[4000]{0:T(1024)S(1)} %copy-done.7, f32[16384,128]{1,0:T(8,128)} %first_total.3.refs_2_, bf16[2016,256]{1,0:T(8,128)(2,1)S(1)} %collective-permute-done.12.refs_3_, ...), custom_call_target="tpu_custom_call" | custom-call | bytes 50000000 | tf_op jit(solution)/shard_map/finish_last/pallas_call | solution.py:415
  (38 shorter events, 0.1 us)
Async XLA Ops:
  11.0 12.4 %copy-start.12 = (s32[9,1000]{1,0:T(8,128)S(1)}, s32[9,1000]{1,0:T(8,128)}, u32[]{:S(2)}) copy-start(s32[9,1000]{1,0:T(8,128)} %get-tuple-element.34) | copy-start | bytes 108004
  11.0 60.8 %collective-permute-start.2 = (bf16[2016,256]{1,0:T(8,128)(2,1)}, bf16[2016,256]{1,0:T(8,128)(2,1)S(1)}, u32[]{:S(2)}, u32[]{:S(2)}) collective-permute-start(bf16[2016,256]{1,0:T(8,128)(2,1)} %get-tuple-element.35), channel_id=1, source_target_pairs={{0,64},{4,68},{8,72},{12,76},{16,80},{20,84},{24,88},{28,92},{32,9... | collective-permute-start | bytes 3096584 | tf_op jit(solution)/shard_map/ppermute | solution.py:532
  15.0 57.9 %copy-start.4 = (f32[64,256]{1,0:T(8,128)S(1)}, f32[64,256]{1,0:T(8,128)}, u32[]{:S(2)}) copy-start(f32[64,256]{1,0:T(8,128)} %refs_11_.1) | copy-start | bytes 196612
  23.2 88.3 %copy-start.10 = (s32[1,1,2]{2,1,0:T(1,128)S(1)}, s32[1,1,2]{2,1,0:T(1,128)}, u32[]{:S(2)}) copy-start(s32[1,1,2]{2,1,0:T(1,128)} %param.15) | copy-start | bytes 28
  23.3 88.9 %copy-start.5 = (s32[4000]{0:T(1024)S(1)}, s32[4000]{0:T(1024)}, u32[]{:S(2)}) copy-start(s32[4000]{0:T(1024)} %reshape_squeeze.14.index_ref.refs_1_) | copy-start | bytes 48004
  23.3 57.9 %collective-permute-start.3 = (bf16[2016,256]{1,0:T(8,128)(2,1)}, bf16[2016,256]{1,0:T(8,128)(2,1)S(1)}, u32[]{:S(2)}, u32[]{:S(2)}) collective-permute-start(bf16[2016,256]{1,0:T(8,128)(2,1)} %shard_map.112), channel_id=1, source_target_pairs={{0,64},{4,68},{8,72},{12,76},{16,80},{20,84},{24,88},{28,92},{32,9... | collective-permute-start | bytes 3096584 | tf_op jit(solution)/shard_map/ppermute | solution.py:532
  23.4 38.1 %collective-permute-start.1 = (s32[9,1000]{1,0:T(8,128)S(1)}, s32[9,1000]{1,0:T(8,128)S(1)}, u32[]{:S(2)}, u32[]{:S(2)}) collective-permute-start(s32[9,1000]{1,0:T(8,128)S(1)} %copy-done.12), channel_id=1, source_target_pairs={{0,64},{4,68},{8,72},{12,76},{16,80},{20,84},{24,88},{28,92},{32,9... | collective-permute-start | bytes 108008 | tf_op jit(solution)/shard_map/ppermute | solution.py:532
  71.8 1.0 copy-start.2
  72.8 1.2 copy-start.3
  80.4 51.1 %copy-start.8 = (f32[64,256]{1,0:T(8,128)S(1)}, f32[64,256]{1,0:T(8,128)}, u32[]{:S(2)}) copy-start(f32[64,256]{1,0:T(8,128)} %refs_12_.1) | copy-start | bytes 196612
  80.4 51.1 %copy-start.9 = (f32[8192]{0:T(1024)S(1)}, f32[8192]{0:T(1024)}, u32[]{:S(2)}) copy-start(f32[8192]{0:T(1024)} %param.9) | copy-start | bytes 98308
  80.4 31.8 %collective-permute-start.4 = (bf16[2016,256]{1,0:T(8,128)(2,1)}, bf16[2016,256]{1,0:T(8,128)(2,1)}, u32[]{:S(2)}, u32[]{:S(2)}) collective-permute-start(bf16[2016,256]{1,0:T(8,128)(2,1)} %get-tuple-element.42), channel_id=1, source_target_pairs={{0,64},{4,68},{8,72},{12,76},{16,80},{20,84},{24,88},{28,92},{32,9... | collective-permute-start | bytes 3096584 | tf_op jit(solution)/shard_map/ppermute | solution.py:532
  82.8 1.4 copy-start
  84.1 47.4 %collective-permute-start.5 = (bf16[2016,256]{1,0:T(8,128)(2,1)}, bf16[2016,256]{1,0:T(8,128)(2,1)S(1)}, u32[]{:S(2)}, u32[]{:S(2)}) collective-permute-start(bf16[2016,256]{1,0:T(8,128)(2,1)} %get-tuple-element.43), channel_id=1, source_target_pairs={{0,64},{4,68},{8,72},{12,76},{16,80},{20,84},{24,88},{28,92},{32,9... | collective-permute-start | bytes 3096584 | tf_op jit(solution)/shard_map/ppermute | solution.py:532
  86.9 65.0 %copy-start.6 = (s32[4000]{0:T(1024)}, s32[4000]{0:T(1024)S(1)}, u32[]{:S(2)}) copy-start(s32[4000]{0:T(1024)S(1)} %reshape_squeeze.13.refs_2_.index_ref.refs_1_) | copy-start | bytes 48004
  107.4 23.2 %collective-permute-start.8 = (f32[64,256]{1,0:T(8,128)S(1)}, f32[64,256]{1,0:T(8,128)S(1)}, u32[]{:S(2)}, u32[]{:S(2)}) collective-permute-start(f32[64,256]{1,0:T(8,128)S(1)} %relation_sum.2.refs_7_), channel_id=1, source_target_pairs={{0,96},{4,100},{8,104},{12,108},{16,112},{20,116},{24,120},{28,124... | collective-permute-start | bytes 196616 | tf_op jit(solution)/shard_map/ppermute | solution.py:532
  107.7 22.8 %collective-permute-start.7 = (f32[64,256]{1,0:T(8,128)S(1)}, f32[64,256]{1,0:T(8,128)S(1)}, u32[]{:S(2)}, u32[]{:S(2)}) collective-permute-start(f32[64,256]{1,0:T(8,128)S(1)} %relation_sum.2.refs_7_), channel_id=1, source_target_pairs={{0,64},{4,68},{8,72},{12,76},{16,80},{20,84},{24,88},{28,92},{32,9... | collective-permute-start | bytes 196616 | tf_op jit(solution)/shard_map/ppermute | solution.py:532
  109.0 22.5 %collective-permute-start.6 = (f32[64,256]{1,0:T(8,128)S(1)}, f32[64,256]{1,0:T(8,128)S(1)}, u32[]{:S(2)}, u32[]{:S(2)}) collective-permute-start(f32[64,256]{1,0:T(8,128)S(1)} %relation_sum.2.refs_7_), channel_id=1, source_target_pairs={{0,32},{4,36},{8,40},{12,44},{16,48},{20,52},{24,56},{28,60},{32,0... | collective-permute-start | bytes 196616 | tf_op jit(solution)/shard_map/ppermute | solution.py:532
  151.9 12.1 %copy-start.11 = (s32[9,1000]{1,0:T(8,128)S(1)}, s32[9,1000]{1,0:T(8,128)}, u32[]{:S(2)}) copy-start(s32[9,1000]{1,0:T(8,128)} %get-tuple-element.33) | copy-start | bytes 108004
  151.9 58.2 %collective-permute-start.9 = (bf16[2016,256]{1,0:T(8,128)(2,1)}, bf16[2016,256]{1,0:T(8,128)(2,1)S(1)}, u32[]{:S(2)}, u32[]{:S(2)}) collective-permute-start(bf16[2016,256]{1,0:T(8,128)(2,1)} %get-tuple-element.45), channel_id=1, source_target_pairs={{0,32},{4,36},{8,40},{12,44},{16,48},{20,52},{24,56},{28,60},{32,0... | collective-permute-start | bytes 3096584 | tf_op jit(solution)/shard_map/ppermute | solution.py:532
  163.9 82.1 %copy-start.7 = (s32[4000]{0:T(1024)S(1)}, s32[4000]{0:T(1024)}, u32[]{:S(2)}) copy-start(s32[4000]{0:T(1024)} %copy-done.6) | copy-start | bytes 48004
  163.9 53.6 %collective-permute-start.10 = (bf16[2016,256]{1,0:T(8,128)(2,1)}, bf16[2016,256]{1,0:T(8,128)(2,1)S(1)}, u32[]{:S(2)}, u32[]{:S(2)}) collective-permute-start(bf16[2016,256]{1,0:T(8,128)(2,1)} %shard_map.114), channel_id=1, source_target_pairs={{0,32},{4,36},{8,40},{12,44},{16,48},{20,52},{24,56},{28,60},{32,0... | collective-permute-start | bytes 3096584 | tf_op jit(solution)/shard_map/ppermute | solution.py:532
  164.0 35.8 %collective-permute-start = (s32[9,1000]{1,0:T(8,128)S(1)}, s32[9,1000]{1,0:T(8,128)S(1)}, u32[]{:S(2)}, u32[]{:S(2)}) collective-permute-start(s32[9,1000]{1,0:T(8,128)S(1)} %copy-done.11), channel_id=1, source_target_pairs={{0,32},{4,36},{8,40},{12,44},{16,48},{20,52},{24,56},{28,60},{32,0... | collective-permute-start | bytes 108008 | tf_op jit(solution)/shard_map/ppermute | solution.py:532
  215.7 30.3 %collective-permute-start.11 = (bf16[2016,256]{1,0:T(8,128)(2,1)S(1)}, bf16[2016,256]{1,0:T(8,128)(2,1)S(1)}, u32[]{:S(2)}, u32[]{:S(2)}) collective-permute-start(bf16[2016,256]{1,0:T(8,128)(2,1)S(1)} %get-tuple-element.53), channel_id=1, source_target_pairs={{0,32},{4,36},{8,40},{12,44},{16,48},{20,52},{24,56},{28,60},{32,0... | collective-permute-start | bytes 3096584 | tf_op jit(solution)/shard_map/ppermute | solution.py:532
  223.0 1.3 copy-start.1
  224.3 42.8 %collective-permute-start.12 = (bf16[2016,256]{1,0:T(8,128)(2,1)S(1)}, bf16[2016,256]{1,0:T(8,128)(2,1)S(1)}, u32[]{:S(2)}, u32[]{:S(2)}) collective-permute-start(bf16[2016,256]{1,0:T(8,128)(2,1)S(1)} %get-tuple-element.54), channel_id=1, source_target_pairs={{0,32},{4,36},{8,40},{12,44},{16,48},{20,52},{24,56},{28,60},{32,0... | collective-permute-start | bytes 3096584 | tf_op jit(solution)/shard_map/ppermute | solution.py:532
  241.8 25.4 %collective-permute-start.15 = (f32[64,256]{1,0:T(8,128)S(1)}, f32[64,256]{1,0:T(8,128)S(1)}, u32[]{:S(2)}, u32[]{:S(2)}) collective-permute-start(f32[64,256]{1,0:T(8,128)S(1)} %relation_sum.3.refs_6_), channel_id=1, source_target_pairs={{0,96},{4,100},{8,104},{12,108},{16,112},{20,116},{24,120},{28,124... | collective-permute-start | bytes 196616 | tf_op jit(solution)/shard_map/ppermute | solution.py:532
  243.8 23.4 %collective-permute-start.14 = (f32[64,256]{1,0:T(8,128)S(1)}, f32[64,256]{1,0:T(8,128)S(1)}, u32[]{:S(2)}, u32[]{:S(2)}) collective-permute-start(f32[64,256]{1,0:T(8,128)S(1)} %relation_sum.3.refs_6_), channel_id=1, source_target_pairs={{0,64},{4,68},{8,72},{12,76},{16,80},{20,84},{24,88},{28,92},{32,9... | collective-permute-start | bytes 196616 | tf_op jit(solution)/shard_map/ppermute | solution.py:532
  245.3 21.8 %collective-permute-start.13 = (f32[64,256]{1,0:T(8,128)S(1)}, f32[64,256]{1,0:T(8,128)S(1)}, u32[]{:S(2)}, u32[]{:S(2)}) collective-permute-start(f32[64,256]{1,0:T(8,128)S(1)} %relation_sum.3.refs_6_), channel_id=1, source_target_pairs={{0,32},{4,36},{8,40},{12,44},{16,48},{20,52},{24,56},{28,60},{32,0... | collective-permute-start | bytes 196616 | tf_op jit(solution)/shard_map/ppermute | solution.py:532
where the time goes:
time: 287 us; the launch traced here: 286 us
  Pallas kernels  177 us (62%)
  waiting for transfers between devices  72.2 us (25%)
  starting transfers between devices  27.2 us (9%)
  local copies, waits for them, and re-layouts  8.24 us (3%)
    ppermute x16, waiting for transfers between devices, from_peer(): lax.ppermute(shard, axis, [(i, i ^ bits) for i in range(lax.axis_size(axi...  72.2 us
    pallas_call x2, Pallas kernels, finish(): pl.pallas_call(body, out_shape=[jax.ShapeDtypeStruct(out_shape, jnp.float...  39 us
    pallas_call x2, Pallas kernels, relation_sum(): pl.pallas_call(functools.partial(relation_kernel, stages), out_shape=jax....  37.8 us
    pallas_call x2, Pallas kernels, first_total(): pl.pallas_call(body, out_shape=jax.ShapeDtypeStruct((2 * row_count, LANES...  36.7 us
    pallas_call x4, Pallas kernels, pack(): pl.pallas_call(body, out_shape=[jax.ShapeDtypeStruct((len(group) * height...  35.8 us
    ppermute x16, starting transfers between devices, from_peer(): lax.ppermute(shard, axis, [(i, i ^ bits) for i in range(lax.axis_size(axi...  27.2 us
    pallas_call x4, Pallas kernels, run_group(): pl.pallas_call(functools.partial(batch_kernel, group, count), out_shape=[...  18.9 us
    pallas_call x1, Pallas kernels, pack_first(): pl.pallas_call(body, out_shape=[jax.ShapeDtypeStruct((2 * row_count, LANE...  8.92 us
  transfers between devices with their start and end apart: 16, of which 4 were waited for; matrix products, arithmetic and copies ran while one was open for 1% of the time, Pallas kernels for 45%

commit v1 on v0

--- a/solution.py
+++ b/solution.py
@@ -289,19 +289,31 @@
 
 
 def first_total(count, groups, row_count, live, other_live, source_index, other_index, own, returned):
+    parts = 8
+    part_rows = 2 * row_count // parts
+    loads = len(own) + len(returned)
+
     def body(live_ref, other_ref, source_ref, index_ref, *refs):
-        own_refs = refs[: len(own)]
-        back_refs = refs[len(own) : len(own) + len(returned)]
-        total, other = refs[len(own) + len(returned) :][:2]
-        rows = refs[len(own) + len(returned) + 2 :]
+        inputs, out_hbm = refs[:loads], refs[loads]
+        buffers = refs[loads + 1 : 2 * loads + 1]
+        rows = refs[2 * loads + 1 : -3]
+        total, other, sems = refs[-3:]
         totals = (total, other)
+        copies = [
+            pltpu.make_async_copy(ref, buffer, sems.at[number])
+            for number, (ref, buffer) in enumerate(zip(inputs, buffers))
+        ]
+        for copy in copies:
+            copy.start()
         total[...] = jnp.zeros_like(total)
         other[...] = jnp.zeros_like(other)
-        for ref, long in zip(back_refs, rows):
-            spread(ref, long)
+        for copy in copies:
+            copy.wait()
+        for buffer, long in zip(buffers[len(own) :], rows):
+            spread(buffer, long)
         scatter_live(
             live_ref,
-            jobs_of(source_ref, 0, own_refs, totals, groups),
+            jobs_of(source_ref, 0, buffers[: len(own)], totals, groups),
             count,
         )
         scatter_live(
@@ -309,15 +321,25 @@
             jobs_of(index_ref, 0, rows, totals, groups),
             count,
         )
-        total[...] += other[...]
+        saves = []
+        for part in range(parts):
+            here = pl.ds(part * part_rows, part_rows)
+            total[here, :] += other[here, :]
+            save = pltpu.make_async_copy(total.at[here], out_hbm.at[here], sems.at[loads + part])
+            save.start()
+            saves.append(save)
+        for save in saves:
+            save.wait()
 
     return pl.pallas_call(
         body,
         out_shape=jax.ShapeDtypeStruct((2 * row_count, LANES), jnp.float32),
-        in_specs=[SMEM] * 4 + [VMEM] * (len(own) + len(returned)),
-        out_specs=VMEM,
-        scratch_shapes=[pltpu.VMEM((2 * row_count, LANES), jnp.float32)]
-        + [pltpu.VMEM(own[0].shape, jnp.float32)] * len(returned),
+        in_specs=[SMEM] * 4 + [ANY] * loads,
+        out_specs=ANY,
+        scratch_shapes=[pltpu.VMEM(array.shape, array.dtype) for array in (*own, *returned)]
+        + [pltpu.VMEM(own[0].shape, jnp.float32)] * len(returned)
+        + [pltpu.VMEM((2 * row_count, LANES), jnp.float32)] * 2
+        + [pltpu.SemaphoreType.DMA((loads + parts,))],
         compiler_params=params(50),
         cost_estimate=cost(60_000_000),
         name="first_total",
@@ -350,7 +372,7 @@
         near_refs = take(len(near))
         rel_ref, rel_state_ref, out_hbm, state_out, new_rel, new_rel_state = take(6)
         next_outs = take(0 if last else 1)
-        total_v, other_v, table_v, state_t, mean_t, sems = take(6)
+        total_v, other_v, third_v, table_v, state_t, mean_t, sems = take(7)
         rows = take(len(returned))
         out_v = refs[0] if last else table_v
         load_total = pltpu.make_async_copy(total_hbm, total_v, sems.at[0])
@@ -358,6 +380,7 @@
         load_total.start()
         load_table.start()
         other_v[...] = jnp.zeros_like(other_v)
+        third_v[...] = jnp.zeros_like(third_v)
         for ref, long in zip(back_refs, rows):
             spread(ref, long)
         rel_total = pair_sum([ref[...] for ref in near_refs])
@@ -367,23 +390,23 @@
         spare = jnp.zeros((LANES - tiles, LANES), jnp.float32)
         state_t[...] = jnp.concatenate([state_ref[...], spare], axis=0).T
         mean_t[...] = jnp.zeros_like(mean_t)
-        load_total.wait()
-        totals = (other_v, total_v)
+        totals = (other_v, third_v)
         scatter_live(
             live_ref,
             jobs_of(index_ref, first, rows, totals, groups),
             count,
         )
+        load_total.wait()
         load_table.wait()
         lane = lax.broadcasted_iota(jnp.int32, (LANES, LANES), 1)
         saves = []
         for step in range(steps):
 
-            @pl.loop(step * step_rows // LANES, (step + 1) * step_rows // LANES)
+            @pl.loop(step * step_rows // LANES, (step + 1) * step_rows // LANES, unroll=4)
             def _(group):
                 base = pl.multiple_of(group * LANES, LANES)
                 sides = [half(base, LANES, side) for side in range(2)]
-                grads = [total_v[side, :] + other_v[side, :] for side in sides]
+                grads = [total_v[side, :] + (other_v[side, :] + third_v[side, :]) for side in sides]
                 square = grads[0] * grads[0] + grads[1] * grads[1]
                 mean = jnp.sum(square, axis=1, keepdims=True) * (1.0 / width)
                 mine = lane == group
@@ -429,6 +452,7 @@
         + [VMEM] * (len(near) + 3),
         out_specs=[HBM] + [VMEM] * (3 + (not last)),
         scratch_shapes=[
+            pltpu.VMEM(table.shape, jnp.float32),
             pltpu.VMEM(table.shape, jnp.float32),
             pltpu.VMEM(table.shape, jnp.float32),
             pltpu.VMEM(table.shape, jnp.float32),

time: 287 us -> 276 us (0.962)
  the two profiles are of different devices: /device:TPU:4 before, /device:TPU:2 now
where the time goes in v1:
time: 276 us
  Pallas kernels  168 us (61%)
  waiting for transfers between devices  73.8 us (27%)
  starting transfers between devices  24.8 us (9%)
  local copies, waits for them, and re-layouts  8.24 us (3%)
    ppermute x16, waiting for transfers between devices, from_peer(): lax.ppermute(shard, axis, [(i, i ^ bits) for i in range(lax.axis_size(axi...  73.8 us
    pallas_call x2, Pallas kernels, relation_sum(): pl.pallas_call(functools.partial(relation_kernel, stages), out_shape=jax....  42.7 us
    pallas_call x4, Pallas kernels, pack(): pl.pallas_call(body, out_shape=[jax.ShapeDtypeStruct((len(group) * height...  35.8 us
    pallas_call x2, Pallas kernels, first_total(): pl.pallas_call(body, out_shape=jax.ShapeDtypeStruct((2 * row_count, LANES...  35 us
    pallas_call x2, Pallas kernels, finish(): pl.pallas_call(body, out_shape=[jax.ShapeDtypeStruct(out_shape, jnp.float...  28.8 us
    ppermute x16, starting transfers between devices, from_peer(): lax.ppermute(shard, axis, [(i, i ^ bits) for i in range(lax.axis_size(axi...  24.8 us
    pallas_call x4, Pallas kernels, run_group(): pl.pallas_call(functools.partial(batch_kernel, group, count), out_shape=[...  16.5 us
    pallas_call x1, Pallas kernels, pack_first(): pl.pallas_call(body, out_shape=[jax.ShapeDtypeStruct((2 * row_count, LANE...  8.92 us
  transfers between devices with their start and end apart: 16, of which 3 were waited for; matrix products, arithmetic and copies ran while one was open for 1% of the time, Pallas kernels for 47%

profile of v1, /device:TPU:2, one launch (start us, length us, event | category | flops | bytes accessed | tf_op | source)
XLA Modules:
  0.0 275.6 jit_solution(8936579524843635690)
XLA Ops:
  0.6 0.7 fusion.2
  1.4 0.7 reshape_squeeze.14.index_ref.refs_1_
  2.1 8.9 %pack_first.1 = (f32[16384,128]{1,0:T(8,128)}, s32[9,1000]{1,0:T(8,128)}, s32[9,1000]{1,0:T(8,128)}, bf16[2016,256]{1,0:T(8,128)(2,1)}) custom-call(s32[4000]{0:T(1024)} %reshape_squeeze.14.index_ref.refs_1_, s32[2]{0:T(128)} %bitcast.12, f32[8192,256]{1,0:T(8,128)} %table_hbm.1, s32[2,4,1000]{2,1,0:T(4,128)} %bitcast.10, s32[2,4,1000]{2,1,0:T(4,128)} %bitcast.11), custom_call_target="tpu_custom_call" | custom-call | bytes 25000000 | tf_op jit(solution)/shard_map/pack_first/pallas_call | solution.py:143
  11.0 0.0 copy-start.12
  11.0 4.0 %collective-permute-start.2 = (bf16[2016,256]{1,0:T(8,128)(2,1)}, bf16[2016,256]{1,0:T(8,128)(2,1)S(1)}, u32[]{:S(2)}, u32[]{:S(2)}) collective-permute-start(bf16[2016,256]{1,0:T(8,128)(2,1)} %get-tuple-element.35), channel_id=1, source_target_pairs={{0,64},{4,68},{8,72},{12,76},{16,80},{20,84},{24,88},{28,92},{32,9... | collective-permute-start | bytes 3096584 | tf_op jit(solution)/shard_map/ppermute | solution.py:556
  15.0 8.3 %shard_map.112 = bf16[2016,256]{1,0:T(8,128)(2,1)} custom-call(s32[4000]{0:T(1024)} %reshape_squeeze.14.index_ref.refs_1_, f32[16384,128]{1,0:T(8,128)} %get-tuple-element.36.table_hbm.refs_5_), custom_call_target="tpu_custom_call" | custom-call | bytes 30000000 | tf_op jit(solution)/shard_map/pallas_call | solution.py:173
  23.2 0.0 copy-start.10
  23.3 0.1 collective-permute-start.3
  23.4 3.5 %collective-permute-start.1 = (s32[9,1000]{1,0:T(8,128)S(1)}, s32[9,1000]{1,0:T(8,128)S(1)}, u32[]{:S(2)}, u32[]{:S(2)}) collective-permute-start(s32[9,1000]{1,0:T(8,128)S(1)} %copy-done.12), channel_id=1, source_target_pairs={{0,64},{4,68},{8,72},{12,76},{16,80},{20,84},{24,88},{28,92},{32,9... | collective-permute-start | bytes 108008 | tf_op jit(solution)/shard_map/ppermute | solution.py:556
  26.9 34.6 %collective-permute-done.1 = s32[9,1000]{1,0:T(8,128)S(1)} collective-permute-done((s32[9,1000]{1,0:T(8,128)S(1)}, s32[9,1000]{1,0:T(8,128)S(1)}, u32[]{:S(2)}, u32[]{:S(2)}) %collective-permute-start.1) | collective-permute-done | bytes 36032 | tf_op jit(solution)/shard_map/ppermute | solution.py:556
  61.5 0.1 reshape.21.index_ref.source_ref
  61.6 9.7 %shard_map.111 = (bf16[2016,256]{1,0:T(8,128)(2,1)S(1)}, bf16[2016,256]{1,0:T(8,128)(2,1)S(1)}) custom-call(s32[4000]{0:T(1024)S(1)} %reshape.21.index_ref.source_ref, f32[16384,128]{1,0:T(8,128)} %get-tuple-element.36.table_hbm.refs_5_), custom_call_target="tpu_custom_call" | custom-call | bytes 30000000 | tf_op jit(solution)/shard_map/pallas_call | solution.py:173
  71.3 0.5 slice.59
  71.9 1.0 copy-done.2
  72.8 1.2 copy-done.3
  74.0 3.9 %batch_terms.4 = (bf16[2016,256]{1,0:T(8,128)(2,1)}, f32[4032,128]{1,0:T(8,128)S(1)}, f32[64,256]{1,0:T(8,128)S(1)}) custom-call(s32[1]{0:T(128)} %bitcast.6.live_ref, s32[2,1024]{1,0:T(2,128)S(1)} %get-tuple-element.71.kind_ref, bf16[2016,256]{1,0:T(8,128)(2,1)S(1)} %copy-done.3, bf16[2016,256]{1,0:T(8,128)(2,1)S(1)} %get-tuple-element.37.target_ref, ...), custom_call_target="tpu_custom_call" | custom-call | bytes 15000000 | tf_op jit(solution)/shard_map/batch_terms/pallas_call | solution.py:271
  78.0 3.2 %collective-permute-start.4 = (bf16[2016,256]{1,0:T(8,128)(2,1)}, bf16[2016,256]{1,0:T(8,128)(2,1)}, u32[]{:S(2)}, u32[]{:S(2)}) collective-permute-start(bf16[2016,256]{1,0:T(8,128)(2,1)} %get-tuple-element.42), channel_id=1, source_target_pairs={{0,64},{4,68},{8,72},{12,76},{16,80},{20,84},{24,88},{28,92},{32,9... | collective-permute-start | bytes 3096584 | tf_op jit(solution)/shard_map/ppermute | solution.py:556
  81.2 1.5 batch_terms.5
  82.8 1.4 copy-done
  84.1 0.3 collective-permute-start.5
  84.4 0.1 reshape_squeeze.13.refs_2_.index_ref.refs_1_
  84.5 24.4 %relation_sum.2.refs_7_ = f32[64,256]{1,0:T(8,128)S(1)} custom-call(f32[64,256]{1,0:T(8,128)S(1)} %get-tuple-element.44.own), custom_call_target="tpu_custom_call" | custom-call | bytes 20000000 | tf_op jit(solution)/shard_map/relation_sum/pallas_call | solution.py:532
  108.9 0.1 collective-permute-start.8
  109.0 0.6 collective-permute-start.7
  109.6 3.5 %collective-permute-start.6 = (f32[64,256]{1,0:T(8,128)S(1)}, f32[64,256]{1,0:T(8,128)S(1)}, u32[]{:S(2)}, u32[]{:S(2)}) collective-permute-start(f32[64,256]{1,0:T(8,128)S(1)} %relation_sum.2.refs_7_), channel_id=1, source_target_pairs={{0,32},{4,36},{8,40},{12,44},{16,48},{20,52},{24,56},{28,60},{32,0... | collective-permute-start | bytes 196616 | tf_op jit(solution)/shard_map/ppermute | solution.py:556
  113.1 0.7 fusion.3
  113.8 14.3 %first_total.2.refs_3_ = f32[16384,128]{1,0:T(8,128)} custom-call(s32[1]{0:T(128)} %bitcast.6.live_ref, s32[1]{0:T(128)} %bitcast.5.other_ref.refs_0_, s32[4000]{0:T(1024)S(1)} %reshape.21.index_ref.source_ref, s32[4000]{0:T(1024)S(1)} %copy-done.5, f32[4032,128]{1,0:T(8,128)S(1)} %get-tuple-element.38.refs_0_, f32[4032,128]{1,0:T(8,128)} %copy-done, ...), custom_call_target="tpu_custom_call" | custom-call | bytes 60000000 | tf_op jit(solution)/shard_map/first_total/pallas_call | solution.py:334
  128.1 2.2 collective-permute-done.8.refs_10_
  130.3 15.6 %finish_next.1 = (f32[16384,128]{1,0:T(8,128)}, f32[64,128]{1,0:T(8,128)S(1)}, f32[64,256]{1,0:T(8,128)S(1)}, f32[64,256]{1,0:T(8,128)S(1)}, bf16[2016,256]{1,0:T(8,128)(2,1)}) custom-call(s32[1]{0:T(128)} %bitcast.5.other_ref.refs_0_, s32[4000]{0:T(1024)S(1)} %copy-done.5, s32[4000]{0:T(1024)S(1)} %reshape_squeeze.13.refs_2_.index_ref.refs_1_, ...), custom_call_target="tpu_custom_call" | custom-call | bytes 50000000 | tf_op jit(solution)/shard_map/finish_next/pallas_call | solution.py:438
  145.9 0.0 copy-start.11
  146.0 1.4 collective-permute-start.9
  147.3 8.1 %shard_map.114 = bf16[2016,256]{1,0:T(8,128)(2,1)} custom-call(s32[4000]{0:T(1024)} %copy-done.6, f32[16384,128]{1,0:T(8,128)} %get-tuple-element.46.table_hbm.refs_4_), custom_call_target="tpu_custom_call" | custom-call | bytes 30000000 | tf_op jit(solution)/shard_map/pallas_call | solution.py:173
  155.5 0.8 collective-permute-start.10
  156.3 1.3 collective-permute-start
  157.6 36.9 %collective-permute-done = s32[9,1000]{1,0:T(8,128)S(1)} collective-permute-done((s32[9,1000]{1,0:T(8,128)S(1)}, s32[9,1000]{1,0:T(8,128)S(1)}, u32[]{:S(2)}, u32[]{:S(2)}) %collective-permute-start) | collective-permute-done | bytes 36032 | tf_op jit(solution)/shard_map/ppermute | solution.py:556
  194.5 0.1 reshape.20.index_ref.source_ref
  194.6 0.5 slice.56
  195.1 9.7 %shard_map.113 = (bf16[2016,256]{1,0:T(8,128)(2,1)S(1)}, bf16[2016,256]{1,0:T(8,128)(2,1)S(1)}) custom-call(s32[4000]{0:T(1024)S(1)} %reshape.20.index_ref.source_ref, f32[16384,128]{1,0:T(8,128)} %get-tuple-element.46.table_hbm.refs_4_), custom_call_target="tpu_custom_call" | custom-call | bytes 30000000 | tf_op jit(solution)/shard_map/pallas_call | solution.py:173
  204.9 5.5 %batch_terms.6 = (bf16[2016,256]{1,0:T(8,128)(2,1)S(1)}, f32[4032,128]{1,0:T(8,128)S(1)}, f32[64,256]{1,0:T(8,128)S(1)}) custom-call(s32[1]{0:T(128)} %bitcast.4.live_ref, s32[2,1024]{1,0:T(2,128)S(1)} %get-tuple-element.69.kind_ref, bf16[2016,256]{1,0:T(8,128)(2,1)S(1)} %collective-permute-done.9.source_ref, ...), custom_call_target="tpu_custom_call" | custom-call | bytes 15000000 | tf_op jit(solution)/shard_map/batch_terms/pallas_call | solution.py:271
  210.4 1.6 collective-permute-start.11
  212.0 5.5 %batch_terms.7 = (bf16[2016,256]{1,0:T(8,128)(2,1)S(1)}, f32[4032,128]{1,0:T(8,128)S(1)}, f32[64,256]{1,0:T(8,128)S(1)}) custom-call(s32[1]{0:T(128)} %bitcast.4.live_ref, s32[2,1024]{1,0:T(2,128)S(1)} %get-tuple-element.68.kind_ref, bf16[2016,256]{1,0:T(8,128)(2,1)S(1)} %collective-permute-done.10.source_ref, ...), custom_call_target="tpu_custom_call" | custom-call | bytes 15000000 | tf_op jit(solution)/shard_map/batch_terms/pallas_call | solution.py:271
  217.5 1.3 copy-done.1
  218.8 18.2 %relation_sum.3.refs_6_ = f32[64,256]{1,0:T(8,128)S(1)} custom-call(f32[64,256]{1,0:T(8,128)S(1)} %get-tuple-element.56.own), custom_call_target="tpu_custom_call" | custom-call | bytes 20000000 | tf_op jit(solution)/shard_map/relation_sum/pallas_call | solution.py:532
  237.1 1.5 collective-permute-start.15
  238.5 1.6 collective-permute-start.14
  240.1 1.4 collective-permute-start.13
  241.5 20.7 %first_total.3.refs_2_ = f32[16384,128]{1,0:T(8,128)} custom-call(s32[1]{0:T(128)} %bitcast.4.live_ref, s32[1]{0:T(128)} %bitcast.other_ref.refs_0_, s32[4000]{0:T(1024)S(1)} %reshape.20.index_ref.source_ref, s32[4000]{0:T(1024)S(1)} %copy-done.7, f32[4032,128]{1,0:T(8,128)S(1)} %get-tuple-element.49.refs_0_, f32[4032,128]{1,0:T(8,128)} %copy-done.1, ...), custom_call_target="tpu_custom_call" | custom-call | bytes 60000000 | tf_op jit(solution)/shard_map/first_total/pallas_call | solution.py:334
  262.2 13.2 %finish_last.1 = (f32[8192,256]{1,0:T(8,128)}, f32[64,128]{1,0:T(8,128)}, f32[64,256]{1,0:T(8,128)}, f32[64,256]{1,0:T(8,128)}) custom-call(s32[1]{0:T(128)} %bitcast.other_ref.refs_0_, s32[4000]{0:T(1024)S(1)} %copy-done.7, f32[16384,128]{1,0:T(8,128)} %first_total.3.refs_2_, bf16[2016,256]{1,0:T(8,128)(2,1)S(1)} %collective-permute-done.12.refs_3_, ...), custom_call_target="tpu_custom_call" | custom-call | bytes 50000000 | tf_op jit(solution)/shard_map/finish_last/pallas_call | solution.py:438
  (38 shorter events, 0.1 us)
Async XLA Ops:
  11.0 12.4 %copy-start.12 = (s32[9,1000]{1,0:T(8,128)S(1)}, s32[9,1000]{1,0:T(8,128)}, u32[]{:S(2)}) copy-start(s32[9,1000]{1,0:T(8,128)} %get-tuple-element.34) | copy-start | bytes 108004
  11.0 60.8 %collective-permute-start.2 = (bf16[2016,256]{1,0:T(8,128)(2,1)}, bf16[2016,256]{1,0:T(8,128)(2,1)S(1)}, u32[]{:S(2)}, u32[]{:S(2)}) collective-permute-start(bf16[2016,256]{1,0:T(8,128)(2,1)} %get-tuple-element.35), channel_id=1, source_target_pairs={{0,64},{4,68},{8,72},{12,76},{16,80},{20,84},{24,88},{28,92},{32,9... | collective-permute-start | bytes 3096584 | tf_op jit(solution)/shard_map/ppermute | solution.py:556
  15.0 57.9 %copy-start.4 = (f32[64,256]{1,0:T(8,128)S(1)}, f32[64,256]{1,0:T(8,128)}, u32[]{:S(2)}) copy-start(f32[64,256]{1,0:T(8,128)} %refs_11_.1) | copy-start | bytes 196612
  23.2 89.8 %copy-start.10 = (s32[1,1,2]{2,1,0:T(1,128)S(1)}, s32[1,1,2]{2,1,0:T(1,128)}, u32[]{:S(2)}) copy-start(s32[1,1,2]{2,1,0:T(1,128)} %param.15) | copy-start | bytes 28
  23.3 90.5 %copy-start.5 = (s32[4000]{0:T(1024)S(1)}, s32[4000]{0:T(1024)}, u32[]{:S(2)}) copy-start(s32[4000]{0:T(1024)} %reshape_squeeze.14.index_ref.refs_1_) | copy-start | bytes 48004
  23.3 58.0 %collective-permute-start.3 = (bf16[2016,256]{1,0:T(8,128)(2,1)}, bf16[2016,256]{1,0:T(8,128)(2,1)S(1)}, u32[]{:S(2)}, u32[]{:S(2)}) collective-permute-start(bf16[2016,256]{1,0:T(8,128)(2,1)} %shard_map.112), channel_id=1, source_target_pairs={{0,64},{4,68},{8,72},{12,76},{16,80},{20,84},{24,88},{28,92},{32,9... | collective-permute-start | bytes 3096584 | tf_op jit(solution)/shard_map/ppermute | solution.py:556
  23.4 38.1 %collective-permute-start.1 = (s32[9,1000]{1,0:T(8,128)S(1)}, s32[9,1000]{1,0:T(8,128)S(1)}, u32[]{:S(2)}, u32[]{:S(2)}) collective-permute-start(s32[9,1000]{1,0:T(8,128)S(1)} %copy-done.12), channel_id=1, source_target_pairs={{0,64},{4,68},{8,72},{12,76},{16,80},{20,84},{24,88},{28,92},{32,9... | collective-permute-start | bytes 108008 | tf_op jit(solution)/shard_map/ppermute | solution.py:556
  71.8 1.0 copy-start.2
  72.8 1.2 copy-start.3
  78.0 52.3 %copy-start.8 = (f32[64,256]{1,0:T(8,128)S(1)}, f32[64,256]{1,0:T(8,128)}, u32[]{:S(2)}) copy-start(f32[64,256]{1,0:T(8,128)} %refs_12_.1) | copy-start | bytes 196612
  78.0 52.4 %copy-start.9 = (f32[8192]{0:T(1024)S(1)}, f32[8192]{0:T(1024)}, u32[]{:S(2)}) copy-start(f32[8192]{0:T(1024)} %param.9) | copy-start | bytes 98308
  78.0 35.8 %collective-permute-start.4 = (bf16[2016,256]{1,0:T(8,128)(2,1)}, bf16[2016,256]{1,0:T(8,128)(2,1)}, u32[]{:S(2)}, u32[]{:S(2)}) collective-permute-start(bf16[2016,256]{1,0:T(8,128)(2,1)} %get-tuple-element.42), channel_id=1, source_target_pairs={{0,64},{4,68},{8,72},{12,76},{16,80},{20,84},{24,88},{28,92},{32,9... | collective-permute-start | bytes 3096584 | tf_op jit(solution)/shard_map/ppermute | solution.py:556
  82.8 1.4 copy-start
  84.1 46.2 %collective-permute-start.5 = (bf16[2016,256]{1,0:T(8,128)(2,1)}, bf16[2016,256]{1,0:T(8,128)(2,1)S(1)}, u32[]{:S(2)}, u32[]{:S(2)}) collective-permute-start(bf16[2016,256]{1,0:T(8,128)(2,1)} %get-tuple-element.43), channel_id=1, source_target_pairs={{0,64},{4,68},{8,72},{12,76},{16,80},{20,84},{24,88},{28,92},{32,9... | collective-permute-start | bytes 3096584 | tf_op jit(solution)/shard_map/ppermute | solution.py:556
  84.5 61.5 %copy-start.6 = (s32[4000]{0:T(1024)}, s32[4000]{0:T(1024)S(1)}, u32[]{:S(2)}) copy-start(s32[4000]{0:T(1024)S(1)} %reshape_squeeze.13.refs_2_.index_ref.refs_1_) | copy-start | bytes 48004
  108.9 21.4 %collective-permute-start.8 = (f32[64,256]{1,0:T(8,128)S(1)}, f32[64,256]{1,0:T(8,128)S(1)}, u32[]{:S(2)}, u32[]{:S(2)}) collective-permute-start(f32[64,256]{1,0:T(8,128)S(1)} %relation_sum.2.refs_7_), channel_id=1, source_target_pairs={{0,96},{4,100},{8,104},{12,108},{16,112},{20,116},{24,120},{28,124... | collective-permute-start | bytes 196616 | tf_op jit(solution)/shard_map/ppermute | solution.py:556
  109.0 21.3 %collective-permute-start.7 = (f32[64,256]{1,0:T(8,128)S(1)}, f32[64,256]{1,0:T(8,128)S(1)}, u32[]{:S(2)}, u32[]{:S(2)}) collective-permute-start(f32[64,256]{1,0:T(8,128)S(1)} %relation_sum.2.refs_7_), channel_id=1, source_target_pairs={{0,64},{4,68},{8,72},{12,76},{16,80},{20,84},{24,88},{28,92},{32,9... | collective-permute-start | bytes 196616 | tf_op jit(solution)/shard_map/ppermute | solution.py:556
  109.6 20.7 %collective-permute-start.6 = (f32[64,256]{1,0:T(8,128)S(1)}, f32[64,256]{1,0:T(8,128)S(1)}, u32[]{:S(2)}, u32[]{:S(2)}) collective-permute-start(f32[64,256]{1,0:T(8,128)S(1)} %relation_sum.2.refs_7_), channel_id=1, source_target_pairs={{0,32},{4,36},{8,40},{12,44},{16,48},{20,52},{24,56},{28,60},{32,0... | collective-permute-start | bytes 196616 | tf_op jit(solution)/shard_map/ppermute | solution.py:556
  145.9 10.3 %copy-start.11 = (s32[9,1000]{1,0:T(8,128)S(1)}, s32[9,1000]{1,0:T(8,128)}, u32[]{:S(2)}) copy-start(s32[9,1000]{1,0:T(8,128)} %get-tuple-element.33) | copy-start | bytes 108004
  146.0 58.9 %collective-permute-start.9 = (bf16[2016,256]{1,0:T(8,128)(2,1)}, bf16[2016,256]{1,0:T(8,128)(2,1)S(1)}, u32[]{:S(2)}, u32[]{:S(2)}) collective-permute-start(bf16[2016,256]{1,0:T(8,128)(2,1)} %get-tuple-element.45), channel_id=1, source_target_pairs={{0,32},{4,36},{8,40},{12,44},{16,48},{20,52},{24,56},{28,60},{32,0... | collective-permute-start | bytes 3096584 | tf_op jit(solution)/shard_map/ppermute | solution.py:556
  155.4 86.0 %copy-start.7 = (s32[4000]{0:T(1024)S(1)}, s32[4000]{0:T(1024)}, u32[]{:S(2)}) copy-start(s32[4000]{0:T(1024)} %copy-done.6) | copy-start | bytes 48004
  155.5 56.5 %collective-permute-start.10 = (bf16[2016,256]{1,0:T(8,128)(2,1)}, bf16[2016,256]{1,0:T(8,128)(2,1)S(1)}, u32[]{:S(2)}, u32[]{:S(2)}) collective-permute-start(bf16[2016,256]{1,0:T(8,128)(2,1)} %shard_map.114), channel_id=1, source_target_pairs={{0,32},{4,36},{8,40},{12,44},{16,48},{20,52},{24,56},{28,60},{32,0... | collective-permute-start | bytes 3096584 | tf_op jit(solution)/shard_map/ppermute | solution.py:556
  156.3 38.2 %collective-permute-start = (s32[9,1000]{1,0:T(8,128)S(1)}, s32[9,1000]{1,0:T(8,128)S(1)}, u32[]{:S(2)}, u32[]{:S(2)}) collective-permute-start(s32[9,1000]{1,0:T(8,128)S(1)} %copy-done.11), channel_id=1, source_target_pairs={{0,32},{4,36},{8,40},{12,44},{16,48},{20,52},{24,56},{28,60},{32,0... | collective-permute-start | bytes 108008 | tf_op jit(solution)/shard_map/ppermute | solution.py:556
  210.4 31.1 %collective-permute-start.11 = (bf16[2016,256]{1,0:T(8,128)(2,1)S(1)}, bf16[2016,256]{1,0:T(8,128)(2,1)S(1)}, u32[]{:S(2)}, u32[]{:S(2)}) collective-permute-start(bf16[2016,256]{1,0:T(8,128)(2,1)S(1)} %get-tuple-element.53), channel_id=1, source_target_pairs={{0,32},{4,36},{8,40},{12,44},{16,48},{20,52},{24,56},{28,60},{32,0... | collective-permute-start | bytes 3096584 | tf_op jit(solution)/shard_map/ppermute | solution.py:556
  217.5 1.3 copy-start.1
  218.8 43.4 %collective-permute-start.12 = (bf16[2016,256]{1,0:T(8,128)(2,1)S(1)}, bf16[2016,256]{1,0:T(8,128)(2,1)S(1)}, u32[]{:S(2)}, u32[]{:S(2)}) collective-permute-start(bf16[2016,256]{1,0:T(8,128)(2,1)S(1)} %get-tuple-element.54), channel_id=1, source_target_pairs={{0,32},{4,36},{8,40},{12,44},{16,48},{20,52},{24,56},{28,60},{32,0... | collective-permute-start | bytes 3096584 | tf_op jit(solution)/shard_map/ppermute | solution.py:556
  237.1 25.1 %collective-permute-start.15 = (f32[64,256]{1,0:T(8,128)S(1)}, f32[64,256]{1,0:T(8,128)S(1)}, u32[]{:S(2)}, u32[]{:S(2)}) collective-permute-start(f32[64,256]{1,0:T(8,128)S(1)} %relation_sum.3.refs_6_), channel_id=1, source_target_pairs={{0,96},{4,100},{8,104},{12,108},{16,112},{20,116},{24,120},{28,124... | collective-permute-start | bytes 196616 | tf_op jit(solution)/shard_map/ppermute | solution.py:556
  238.5 23.6 %collective-permute-start.14 = (f32[64,256]{1,0:T(8,128)S(1)}, f32[64,256]{1,0:T(8,128)S(1)}, u32[]{:S(2)}, u32[]{:S(2)}) collective-permute-start(f32[64,256]{1,0:T(8,128)S(1)} %relation_sum.3.refs_6_), channel_id=1, source_target_pairs={{0,64},{4,68},{8,72},{12,76},{16,80},{20,84},{24,88},{28,92},{32,9... | collective-permute-start | bytes 196616 | tf_op jit(solution)/shard_map/ppermute | solution.py:556
  240.1 22.1 %collective-permute-start.13 = (f32[64,256]{1,0:T(8,128)S(1)}, f32[64,256]{1,0:T(8,128)S(1)}, u32[]{:S(2)}, u32[]{:S(2)}) collective-permute-start(f32[64,256]{1,0:T(8,128)S(1)} %relation_sum.3.refs_6_), channel_id=1, source_target_pairs={{0,32},{4,36},{8,40},{12,44},{16,48},{20,52},{24,56},{28,60},{32,0... | collective-permute-start | bytes 196616 | tf_op jit(solution)/shard_map/ppermute | solution.py:556

commit v2 on v1

--- a/solution.py
+++ b/solution.py
@@ -18,8 +18,9 @@
 VMEM = pl.BlockSpec(memory_space=pltpu.VMEM)
 ANY = pl.BlockSpec(memory_space=pl.ANY)
 HBM = pl.BlockSpec(memory_space=pltpu.HBM)
-GATHER_UNROLL = 20
+GATHER_UNROLL = 40
 SCATTER_UNROLL = 8
+UPDATE_UNROLL = 8
 BLOCK = 256
 LANES = 128
 MIB = 1024 * 1024
@@ -370,7 +371,9 @@
         back_refs = take(len(returned))
         table_hbm, state_ref = take(2)
         near_refs = take(len(near))
-        rel_ref, rel_state_ref, out_hbm, state_out, new_rel, new_rel_state = take(6)
+        rel_refs = take(2 if last else 0)
+        out_hbm, state_out = take(2)
+        new_rel_refs = take(2 if last else 0)
         next_outs = take(0 if last else 1)
         total_v, other_v, third_v, table_v, state_t, mean_t, sems = take(7)
         rows = take(len(returned))
@@ -383,10 +386,11 @@
         third_v[...] = jnp.zeros_like(third_v)
         for ref, long in zip(back_refs, rows):
             spread(ref, long)
-        rel_total = pair_sum([ref[...] for ref in near_refs])
-        rel_new = rel_state_ref[...] + rel_total * rel_total
-        new_rel_state[...] = rel_new
-        new_rel[...] = rel_ref[...] - rel_rate * rel_total / jnp.sqrt(rel_new)
+        if last:
+            rel_total = pair_sum([ref[...] for ref in near_refs])
+            rel_new = rel_refs[1][...] + rel_total * rel_total
+            new_rel_refs[1][...] = rel_new
+            new_rel_refs[0][...] = rel_refs[0][...] - rel_rate * rel_total / jnp.sqrt(rel_new)
         spare = jnp.zeros((LANES - tiles, LANES), jnp.float32)
         state_t[...] = jnp.concatenate([state_ref[...], spare], axis=0).T
         mean_t[...] = jnp.zeros_like(mean_t)
@@ -402,7 +406,7 @@
         saves = []
         for step in range(steps):
 
-            @pl.loop(step * step_rows // LANES, (step + 1) * step_rows // LANES, unroll=4)
+            @pl.loop(step * step_rows // LANES, (step + 1) * step_rows // LANES, unroll=UPDATE_UNROLL)
             def _(group):
                 base = pl.multiple_of(group * LANES, LANES)
                 sides = [half(base, LANES, side) for side in range(2)]
@@ -440,17 +444,16 @@
         out_shape=[
             jax.ShapeDtypeStruct(out_shape, jnp.float32),
             jax.ShapeDtypeStruct((tiles, LANES), jnp.float32),
-            rel_shape,
-            rel_shape,
         ]
+        + [rel_shape] * (2 * last)
         + [jax.ShapeDtypeStruct((len(next_batches) * round_up(count, 16), width), jnp.bfloat16)]
         * (not last),
         in_specs=[SMEM] * len(indices)
         + [ANY]
         + [VMEM] * len(returned)
         + [HBM]
-        + [VMEM] * (len(near) + 3),
-        out_specs=[HBM] + [VMEM] * (3 + (not last)),
+        + [VMEM] * (1 + len(near) + 2 * last),
+        out_specs=[HBM] + [VMEM] * (1 + 2 * last + (not last)),
         scratch_shapes=[
             pltpu.VMEM(table.shape, jnp.float32),
             pltpu.VMEM(table.shape, jnp.float32),
@@ -465,7 +468,7 @@
         compiler_params=params(50),
         cost_estimate=cost(50_000_000),
         name="finish_last" if last else "finish_next",
-    )(*indices, total, *returned, table, state, *near, relations, rel_state)
+    )(*indices, total, *returned, table, state, *near, *((relations, rel_state) if last else ()))
 
 
 def flip(index, bits):
@@ -476,8 +479,8 @@
     return index
 
 
-def relation_kernel(stages, own, summed, *scratch):
-    parts, received = (own,) + scratch[:-3], scratch[-3]
+def relation_kernel(stages, near, finish, *scratch):
+    parts, received = scratch[:-3], scratch[-3]
     send_sems, recv_sems = scratch[-2:]
     dom, rep = lax.axis_index("dom"), lax.axis_index("rep")
 
@@ -491,6 +494,7 @@
             barrier, inc=1, device_id=device(peer), device_id_type=pl.DeviceIdType.MESH
         )
     pl.semaphore_wait(barrier, len(peers))
+    parts[0][...] = pair_sum([ref[...] for ref in near])
     slot = 0
     for number, stage in enumerate(stages):
         copies = []
@@ -512,7 +516,7 @@
         total = pair_sum([parts[number][...]] + [received[first + i] for i in range(len(stage))])
         if number + 1 < len(stages):
             parts[number + 1][...] = total
-    summed[...] = total
+    finish(total)
 
 
 def pair_sum(values):
@@ -521,31 +525,59 @@
     return values[0]
 
 
-def relation_sum(rel_grad):
-    stages = [
-        [(0, 1), (0, 2), (0, 3)],
-        [(1, 0), (2, 0), (3, 0)],
-        [(4, 0)],
-    ]
-    slots = sum(len(stage) for stage in stages)
-    shape = rel_grad.shape
+def relation_call(body, inputs, outputs, collective_id):
+    slots = sum(len(stage) for stage in STAGES)
+    shape = inputs[0].shape
     return pl.pallas_call(
-        functools.partial(relation_kernel, stages),
-        out_shape=jax.ShapeDtypeStruct(shape, jnp.float32),
-        in_specs=[VMEM],
-        out_specs=VMEM,
-        scratch_shapes=[pltpu.VMEM(shape, jnp.float32)] * (len(stages) - 1)
+        body,
+        out_shape=[jax.ShapeDtypeStruct(shape, jnp.float32)] * outputs,
+        in_specs=[VMEM] * len(inputs),
+        out_specs=[VMEM] * outputs,
+        scratch_shapes=[pltpu.VMEM(shape, jnp.float32)] * len(STAGES)
         + [
             pltpu.VMEM((slots,) + shape, jnp.float32),
             pltpu.SemaphoreType.DMA((slots,)),
             pltpu.SemaphoreType.DMA((slots,)),
         ],
         compiler_params=pltpu.CompilerParams(
-            collective_id=0, has_side_effects=True, vmem_limit_bytes=4 * MIB
+            collective_id=collective_id, has_side_effects=True, vmem_limit_bytes=4 * MIB
         ),
         cost_estimate=cost(20_000_000),
-        name="relation_sum",
-    )(rel_grad)
+    )(*inputs)
+
+
+STAGES = (
+    ((0, 1), (0, 2), (0, 3)),
+    ((1, 0), (2, 0), (3, 0)),
+    ((4, 0),),
+)
+
+
+def relation_sum(rel_grad):
+    def body(own, summed, *scratch):
+        def finish(total):
+            summed[...] = total
+
+        relation_kernel(STAGES, [own], finish, *scratch)
+
+    return relation_call(body, [rel_grad], 1, 0)[0]
+
+
+def relation_step(near, relations, rel_state):
+    count = len(near)
+
+    def body(*refs):
+        near_refs = refs[:count]
+        rel_ref, state_ref, new_rel, new_state = refs[count : count + 4]
+
+        def finish(total):
+            state = state_ref[...] + total * total
+            new_state[...] = state
+            new_rel[...] = rel_ref[...] - rel_rate * total / jnp.sqrt(state)
+
+        relation_kernel(STAGES, near_refs, finish, *refs[count + 4 :])
+
+    return relation_call(body, [*near, relations, rel_state], 2, 1)
 
 
 def from_partner(shard, axis, distance):
@@ -589,6 +621,9 @@
             note[batches : 2 * batches], ((0, 0), (0, padded - count)), constant_values=-1
         )
         targets = pack(other_index, table, groups, count, width, 50)
+        if number:
+            near, targets = lax.optimization_barrier((near, targets))
+            relations, rel_state = relation_step(near, relations, rel_state)
         rel_grad = jnp.zeros(relations.shape, jnp.float32)
         own, returned = [], []
         for place, group in enumerate(groups):
@@ -604,14 +639,16 @@
             )
             own.append(grad_target)
             returned.append(from_partner(grad_source, "dom", swap_bit))
-        near = [relation_sum(rel_grad)]
+        if last:
+            rel_grad = relation_sum(rel_grad)
+        near = [rel_grad]
         for bits in (8, 16, 24):
-            near.append(from_peer(near[0], "dom", bits))
+            near.append(from_peer(rel_grad, "dom", bits))
         early = len(groups) - 1
         total = first_total(
             count, groups, row_count, other_live, live, other_index, source_index, own, returned[:early]
         )
-        table, state, relations, rel_state, *sent = finish(
+        table, state, *more = finish(
             count,
             groups,
             live,
@@ -622,12 +659,16 @@
             table,
             state,
             width,
-            near,
+            near if last else (),
             relations,
             rel_state,
             None if last else sources[number + 1],
             () if last else groups[0],
         )
+        if last:
+            relations, rel_state = more
+        else:
+            sent = more
     return (table, state.reshape(row_count), relations, rel_state)
 
 

time: 276 us -> 292 us (1.058)
  waiting for transfers between devices: 73.8 us -> 101 us
  Pallas kernels: 168 us -> 158 us
    ppermute x16, waiting for transfers between devices: 73.8 us -> 101 us  [from_peer(): lax.ppermute(shard, axis, [(i, i ^ bits) for i in range(lax.axis_size(axi...]
    pallas_call x2, Pallas kernels: 42.7 us -> 35.1 us  [relation_call(): pl.pallas_call(body, out_shape=[jax.ShapeDtypeStruct(shape, jnp.float32)]...]
  transfers between devices with their start and end apart: 16 -> 16, of which waited for: 3 -> 4; matrix products, arithmetic and copies ran while one was open for 1% -> 1% of each run, Pallas kernels for 47% -> 42%
where the time goes in v2:
time: 292 us; the launch traced here: 291 us
  Pallas kernels  158 us (54%)
  waiting for transfers between devices  101 us (35%)
  starting transfers between devices  22.9 us (8%)
  local copies, waits for them, and re-layouts  8.22 us (3%)
    ppermute x16, waiting for transfers between devices, from_peer(): lax.ppermute(shard, axis, [(i, i ^ bits) for i in range(lax.axis_size(axi...  101 us
    pallas_call x2, Pallas kernels, relation_call(): pl.pallas_call(body, out_shape=[jax.ShapeDtypeStruct(shape, jnp.float32)]...  35.1 us
    pallas_call x2, Pallas kernels, first_total(): pl.pallas_call(body, out_shape=jax.ShapeDtypeStruct((2 * row_count, LANES...  34.8 us
    pallas_call x4, Pallas kernels, pack(): pl.pallas_call(body, out_shape=[jax.ShapeDtypeStruct((len(group) * height...  34.6 us
    pallas_call x2, Pallas kernels, finish(): pl.pallas_call(body, out_shape=[jax.ShapeDtypeStruct(out_shape, jnp.float...  27.3 us
    ppermute x16, starting transfers between devices, from_peer(): lax.ppermute(shard, axis, [(i, i ^ bits) for i in range(lax.axis_size(axi...  22.9 us
    pallas_call x4, Pallas kernels, run_group(): pl.pallas_call(functools.partial(batch_kernel, group, count), out_shape=[...  16.8 us
    pallas_call x1, Pallas kernels, pack_first(): pl.pallas_call(body, out_shape=[jax.ShapeDtypeStruct((2 * row_count, LANE...  8.93 us
  transfers between devices with their start and end apart: 16, of which 4 were waited for; matrix products, arithmetic and copies ran while one was open for 1% of the time, Pallas kernels for 42%

profile of v2, /device:TPU:2, one launch (start us, length us, event | category | flops | bytes accessed | tf_op | source)
XLA Modules:
  0.0 291.0 jit_solution(12004231366150133628)
XLA Ops:
  0.6 0.7 fusion.2
  1.4 0.7 reshape_squeeze.14.index_ref.refs_1_
  2.1 8.9 %pack_first.1 = (f32[16384,128]{1,0:T(8,128)}, s32[9,1000]{1,0:T(8,128)}, s32[9,1000]{1,0:T(8,128)}, bf16[2016,256]{1,0:T(8,128)(2,1)}) custom-call(s32[4000]{0:T(1024)} %reshape_squeeze.14.index_ref.refs_1_, s32[2]{0:T(128)} %bitcast.12, f32[8192,256]{1,0:T(8,128)} %table_hbm.1, s32[2,4,1000]{2,1,0:T(4,128)} %bitcast.10, s32[2,4,1000]{2,1,0:T(4,128)} %bitcast.11), custom_call_target="tpu_custom_call" | custom-call | bytes 25000000 | tf_op jit(solution)/shard_map/pack_first/pallas_call | solution.py:144
  11.0 4.0 %collective-permute-start.2 = (bf16[2016,256]{1,0:T(8,128)(2,1)}, bf16[2016,256]{1,0:T(8,128)(2,1)S(1)}, u32[]{:S(2)}, u32[]{:S(2)}) collective-permute-start(bf16[2016,256]{1,0:T(8,128)(2,1)} %get-tuple-element.41), channel_id=1, source_target_pairs={{0,64},{4,68},{8,72},{12,76},{16,80},{20,84},{24,88},{28,92},{32,9... | collective-permute-start | bytes 3096584 | tf_op jit(solution)/shard_map/ppermute | solution.py:588
  15.0 8.0 %shard_map.112 = bf16[2016,256]{1,0:T(8,128)(2,1)} custom-call(s32[4000]{0:T(1024)} %reshape_squeeze.14.index_ref.refs_1_, f32[16384,128]{1,0:T(8,128)} %get-tuple-element.42.table_hbm.refs_5_), custom_call_target="tpu_custom_call" | custom-call | bytes 30000000 | tf_op jit(solution)/shard_map/pallas_call | solution.py:174
  23.0 0.0 copy-start.10
  23.0 0.1 collective-permute-start.3
  23.1 3.5 %collective-permute-start.1 = (s32[9,1000]{1,0:T(8,128)S(1)}, s32[9,1000]{1,0:T(8,128)S(1)}, u32[]{:S(2)}, u32[]{:S(2)}) collective-permute-start(s32[9,1000]{1,0:T(8,128)S(1)} %copy-done.12), channel_id=1, source_target_pairs={{0,64},{4,68},{8,72},{12,76},{16,80},{20,84},{24,88},{28,92},{32,9... | collective-permute-start | bytes 108008 | tf_op jit(solution)/shard_map/ppermute | solution.py:588
  26.6 34.9 %collective-permute-done.1 = s32[9,1000]{1,0:T(8,128)S(1)} collective-permute-done((s32[9,1000]{1,0:T(8,128)S(1)}, s32[9,1000]{1,0:T(8,128)S(1)}, u32[]{:S(2)}, u32[]{:S(2)}) %collective-permute-start.1) | collective-permute-done | bytes 36032 | tf_op jit(solution)/shard_map/ppermute | solution.py:588
  61.5 0.1 reshape.21.index_ref.source_ref
  61.6 9.3 %shard_map.111 = (bf16[2016,256]{1,0:T(8,128)(2,1)S(1)}, bf16[2016,256]{1,0:T(8,128)(2,1)S(1)}) custom-call(s32[4000]{0:T(1024)S(1)} %reshape.21.index_ref.source_ref, f32[16384,128]{1,0:T(8,128)} %get-tuple-element.42.table_hbm.refs_5_), custom_call_target="tpu_custom_call" | custom-call | bytes 30000000 | tf_op jit(solution)/shard_map/pallas_call | solution.py:174
  70.9 0.5 slice.59
  71.5 1.0 copy-done.2
  72.4 1.2 copy-done.3
  73.7 4.0 %batch_terms.4 = (bf16[2016,256]{1,0:T(8,128)(2,1)}, f32[4032,128]{1,0:T(8,128)S(1)}, f32[64,256]{1,0:T(8,128)S(1)}) custom-call(s32[1]{0:T(128)} %bitcast.6.live_ref, s32[2,1024]{1,0:T(2,128)S(1)} %get-tuple-element.83.kind_ref, bf16[2016,256]{1,0:T(8,128)(2,1)S(1)} %copy-done.3, bf16[2016,256]{1,0:T(8,128)(2,1)S(1)} %get-tuple-element.43.target_ref, ...), custom_call_target="tpu_custom_call" | custom-call | bytes 15000000 | tf_op jit(solution)/shard_map/batch_terms/pallas_call | solution.py:272
  77.7 3.2 %collective-permute-start.4 = (bf16[2016,256]{1,0:T(8,128)(2,1)}, bf16[2016,256]{1,0:T(8,128)(2,1)}, u32[]{:S(2)}, u32[]{:S(2)}) collective-permute-start(bf16[2016,256]{1,0:T(8,128)(2,1)} %get-tuple-element.48), channel_id=1, source_target_pairs={{0,64},{4,68},{8,72},{12,76},{16,80},{20,84},{24,88},{28,92},{32,9... | collective-permute-start | bytes 3096584 | tf_op jit(solution)/shard_map/ppermute | solution.py:588
  80.9 1.6 batch_terms.5
  82.5 1.3 copy-done.1
  83.9 0.3 collective-permute-start.5
  84.1 0.1 reshape_squeeze.13.refs_2_.index_ref.refs_1_
  84.2 0.6 fusion.3
  84.8 19.9 %collective-permute-done.4.refs_2_ = bf16[2016,256]{1,0:T(8,128)(2,1)} collective-permute-done((bf16[2016,256]{1,0:T(8,128)(2,1)}, bf16[2016,256]{1,0:T(8,128)(2,1)}, u32[]{:S(2)}, u32[]{:S(2)}) %collective-permute-start.4) | collective-permute-done | bytes 1032224 | tf_op jit(solution)/shard_map/ppermute | solution.py:588
  104.7 14.2 %first_total.2.refs_3_ = f32[16384,128]{1,0:T(8,128)} custom-call(s32[1]{0:T(128)} %bitcast.6.live_ref, s32[1]{0:T(128)} %bitcast.5.other_ref.refs_0_, s32[4000]{0:T(1024)S(1)} %reshape.21.index_ref.source_ref, s32[4000]{0:T(1024)S(1)} %copy-done.5, f32[4032,128]{1,0:T(8,128)S(1)} %get-tuple-element.44.refs_0_, f32[4032,128]{1,0:T(8,128)} %copy-done.1, ...), custom_call_target="tpu_custom_call" | custom-call | bytes 60000000 | tf_op jit(solution)/shard_map/first_total/pallas_call | solution.py:335
  118.9 7.8 %collective-permute-done.5.refs_4_ = bf16[2016,256]{1,0:T(8,128)(2,1)S(1)} collective-permute-done((bf16[2016,256]{1,0:T(8,128)(2,1)}, bf16[2016,256]{1,0:T(8,128)(2,1)S(1)}, u32[]{:S(2)}, u32[]{:S(2)}) %collective-permute-start.5) | collective-permute-done | bytes 1032224 | tf_op jit(solution)/shard_map/ppermute | solution.py:588
  126.7 14.8 %finish_next.1 = (f32[16384,128]{1,0:T(8,128)}, f32[64,128]{1,0:T(8,128)S(1)}, bf16[2016,256]{1,0:T(8,128)(2,1)}) custom-call(s32[1]{0:T(128)} %bitcast.5.other_ref.refs_0_, s32[4000]{0:T(1024)S(1)} %copy-done.5, s32[4000]{0:T(1024)S(1)} %reshape_squeeze.13.refs_2_.index_ref.refs_1_, f32[16384,128]{1,0:T(8,128)} %first_total.2.refs_3_, ...), custom_call_target="tpu_custom_call" | custom-call | bytes 50000000 | tf_op jit(solution)/shard_map/finish_next/pallas_call | solution.py:442
  141.5 0.0 copy-start.11
  141.6 0.1 collective-permute-start.6
  141.7 8.0 %shard_map.115 = bf16[2016,256]{1,0:T(8,128)(2,1)} custom-call(s32[4000]{0:T(1024)} %copy-done.6, f32[16384,128]{1,0:T(8,128)} %get-tuple-element.52.table_hbm.refs_4_), custom_call_target="tpu_custom_call" | custom-call | bytes 30000000 | tf_op jit(solution)/shard_map/pallas_call | solution.py:174
  149.7 2.1 collective-permute-start.10
  151.8 0.1 collective-permute-start
  151.9 38.5 %collective-permute-done = s32[9,1000]{1,0:T(8,128)S(1)} collective-permute-done((s32[9,1000]{1,0:T(8,128)S(1)}, s32[9,1000]{1,0:T(8,128)S(1)}, u32[]{:S(2)}, u32[]{:S(2)}) %collective-permute-start) | collective-permute-done | bytes 36032 | tf_op jit(solution)/shard_map/ppermute | solution.py:588
  190.4 0.1 reshape.20.index_ref.source_ref
  190.5 0.5 slice.56
  191.0 0.3 collective-permute-start.7
  191.3 3.2 %collective-permute-start.8 = (f32[64,256]{1,0:T(8,128)S(1)}, f32[64,256]{1,0:T(8,128)S(1)}, u32[]{:S(2)}, u32[]{:S(2)}) collective-permute-start(f32[64,256]{1,0:T(8,128)S(1)} %get-tuple-element.56.refs_0_), channel_id=1, source_target_pairs={{0,64},{4,68},{8,72},{12,76},{16,80},{20,84},{24,88},{28,92},{32,9... | collective-permute-start | bytes 196616 | tf_op jit(solution)/shard_map/ppermute | solution.py:588
  194.5 1.2 collective-permute-start.9
  195.7 9.3 %shard_map.113 = (bf16[2016,256]{1,0:T(8,128)(2,1)S(1)}, bf16[2016,256]{1,0:T(8,128)(2,1)S(1)}) custom-call(s32[4000]{0:T(1024)S(1)} %reshape.20.index_ref.source_ref, f32[16384,128]{1,0:T(8,128)} %get-tuple-element.52.table_hbm.refs_4_), custom_call_target="tpu_custom_call" | custom-call | bytes 30000000 | tf_op jit(solution)/shard_map/pallas_call | solution.py:174
  205.0 17.2 %shard_map.114 = (f32[64,256]{1,0:T(8,128)S(1)}, f32[64,256]{1,0:T(8,128)S(1)}) custom-call(f32[64,256]{1,0:T(8,128)S(1)} %get-tuple-element.56.refs_0_, f32[64,256]{1,0:T(8,128)S(1)} %collective-permute-done.7.refs_1_, f32[64,256]{1,0:T(8,128)S(1)} %collective-permute-done.8.refs_2_, f32[64,256]{1,0:T(8,128)S(1)} %collective-permute-done.9.refs_3_, ...), custom_call_target="tpu_custom_call" | custom-call | bytes 20000000 | tf_op jit(solution)/shard_map/pallas_call | solution.py:531
  222.2 5.5 %batch_terms.6 = (bf16[2016,256]{1,0:T(8,128)(2,1)S(1)}, f32[4032,128]{1,0:T(8,128)S(1)}, f32[64,256]{1,0:T(8,128)S(1)}) custom-call(s32[1]{0:T(128)} %bitcast.4.live_ref, s32[2,1024]{1,0:T(2,128)S(1)} %get-tuple-element.81.kind_ref, bf16[2016,256]{1,0:T(8,128)(2,1)S(1)} %collective-permute-done.6.source_ref, ...), custom_call_target="tpu_custom_call" | custom-call | bytes 15000000 | tf_op jit(solution)/shard_map/batch_terms/pallas_call | solution.py:272
  227.7 0.1 collective-permute-start.11
  227.8 5.7 %batch_terms.7 = (bf16[2016,256]{1,0:T(8,128)(2,1)S(1)}, f32[4032,128]{1,0:T(8,128)S(1)}, f32[64,256]{1,0:T(8,128)S(1)}) custom-call(s32[1]{0:T(128)} %bitcast.4.live_ref, s32[2,1024]{1,0:T(2,128)S(1)} %get-tuple-element.80.kind_ref, bf16[2016,256]{1,0:T(8,128)(2,1)S(1)} %collective-permute-done.10.source_ref, ...), custom_call_target="tpu_custom_call" | custom-call | bytes 15000000 | tf_op jit(solution)/shard_map/batch_terms/pallas_call | solution.py:272
  233.6 1.3 copy-done
  234.9 17.9 %shard_map.116.refs_6_ = f32[64,256]{1,0:T(8,128)S(1)} custom-call(f32[64,256]{1,0:T(8,128)S(1)} %get-tuple-element.68.own), custom_call_target="tpu_custom_call" | custom-call | bytes 20000000 | tf_op jit(solution)/shard_map/pallas_call | solution.py:531
  252.8 0.1 collective-permute-start.13
  252.9 2.3 collective-permute-start.14
  255.2 2.4 collective-permute-start.15
  257.6 20.6 %first_total.3.refs_2_ = f32[16384,128]{1,0:T(8,128)} custom-call(s32[1]{0:T(128)} %bitcast.4.live_ref, s32[1]{0:T(128)} %bitcast.other_ref.refs_0_, s32[4000]{0:T(1024)S(1)} %reshape.20.index_ref.source_ref, s32[4000]{0:T(1024)S(1)} %copy-done.7, f32[4032,128]{1,0:T(8,128)S(1)} %get-tuple-element.61.refs_0_, f32[4032,128]{1,0:T(8,128)} %copy-done, ...), custom_call_target="tpu_custom_call" | custom-call | bytes 60000000 | tf_op jit(solution)/shard_map/first_total/pallas_call | solution.py:335
  278.3 12.5 %finish_last.1 = (f32[8192,256]{1,0:T(8,128)}, f32[64,128]{1,0:T(8,128)}, f32[64,256]{1,0:T(8,128)}, f32[64,256]{1,0:T(8,128)}) custom-call(s32[1]{0:T(128)} %bitcast.other_ref.refs_0_, s32[4000]{0:T(1024)S(1)} %copy-done.7, f32[16384,128]{1,0:T(8,128)} %first_total.3.refs_2_, bf16[2016,256]{1,0:T(8,128)(2,1)S(1)} %collective-permute-done.12.refs_3_, ...), custom_call_target="tpu_custom_call" | custom-call | bytes 50000000 | tf_op jit(solution)/shard_map/finish_last/pallas_call | solution.py:442
  (38 shorter events, 0.1 us)
Async XLA Ops:
  11.0 12.1 %copy-start.12 = (s32[9,1000]{1,0:T(8,128)S(1)}, s32[9,1000]{1,0:T(8,128)}, u32[]{:S(2)}) copy-start(s32[9,1000]{1,0:T(8,128)} %get-tuple-element.40) | copy-start | bytes 108004
  11.0 60.4 %collective-permute-start.2 = (bf16[2016,256]{1,0:T(8,128)(2,1)}, bf16[2016,256]{1,0:T(8,128)(2,1)S(1)}, u32[]{:S(2)}, u32[]{:S(2)}) collective-permute-start(bf16[2016,256]{1,0:T(8,128)(2,1)} %get-tuple-element.41), channel_id=1, source_target_pairs={{0,64},{4,68},{8,72},{12,76},{16,80},{20,84},{24,88},{28,92},{32,9... | collective-permute-start | bytes 3096584 | tf_op jit(solution)/shard_map/ppermute | solution.py:588
  15.0 57.5 %copy-start.4 = (f32[64,256]{1,0:T(8,128)S(1)}, f32[64,256]{1,0:T(8,128)}, u32[]{:S(2)}) copy-start(f32[64,256]{1,0:T(8,128)} %refs_4_.1) | copy-start | bytes 196612
  23.0 61.2 %copy-start.10 = (s32[1,1,2]{2,1,0:T(1,128)S(1)}, s32[1,1,2]{2,1,0:T(1,128)}, u32[]{:S(2)}) copy-start(s32[1,1,2]{2,1,0:T(1,128)} %param.15) | copy-start | bytes 28
  23.0 81.7 %copy-start.5 = (s32[4000]{0:T(1024)S(1)}, s32[4000]{0:T(1024)}, u32[]{:S(2)}) copy-start(s32[4000]{0:T(1024)} %reshape_squeeze.14.index_ref.refs_1_) | copy-start | bytes 48004
  23.0 57.9 %collective-permute-start.3 = (bf16[2016,256]{1,0:T(8,128)(2,1)}, bf16[2016,256]{1,0:T(8,128)(2,1)S(1)}, u32[]{:S(2)}, u32[]{:S(2)}) collective-permute-start(bf16[2016,256]{1,0:T(8,128)(2,1)} %shard_map.112), channel_id=1, source_target_pairs={{0,64},{4,68},{8,72},{12,76},{16,80},{20,84},{24,88},{28,92},{32,9... | collective-permute-start | bytes 3096584 | tf_op jit(solution)/shard_map/ppermute | solution.py:588
  23.1 38.4 %collective-permute-start.1 = (s32[9,1000]{1,0:T(8,128)S(1)}, s32[9,1000]{1,0:T(8,128)S(1)}, u32[]{:S(2)}, u32[]{:S(2)}) collective-permute-start(s32[9,1000]{1,0:T(8,128)S(1)} %copy-done.12), channel_id=1, source_target_pairs={{0,64},{4,68},{8,72},{12,76},{16,80},{20,84},{24,88},{28,92},{32,9... | collective-permute-start | bytes 108008 | tf_op jit(solution)/shard_map/ppermute | solution.py:588
  71.4 1.0 copy-start.2
  72.4 1.2 copy-start.3
  77.7 49.1 %copy-start.9 = (f32[8192]{0:T(1024)S(1)}, f32[8192]{0:T(1024)}, u32[]{:S(2)}) copy-start(f32[8192]{0:T(1024)} %param.9) | copy-start | bytes 98308
  77.7 27.0 %collective-permute-start.4 = (bf16[2016,256]{1,0:T(8,128)(2,1)}, bf16[2016,256]{1,0:T(8,128)(2,1)}, u32[]{:S(2)}, u32[]{:S(2)}) collective-permute-start(bf16[2016,256]{1,0:T(8,128)(2,1)} %get-tuple-element.48), channel_id=1, source_target_pairs={{0,64},{4,68},{8,72},{12,76},{16,80},{20,84},{24,88},{28,92},{32,9... | collective-permute-start | bytes 3096584 | tf_op jit(solution)/shard_map/ppermute | solution.py:588
  82.5 1.3 copy-start.1
  83.9 42.9 %collective-permute-start.5 = (bf16[2016,256]{1,0:T(8,128)(2,1)}, bf16[2016,256]{1,0:T(8,128)(2,1)S(1)}, u32[]{:S(2)}, u32[]{:S(2)}) collective-permute-start(bf16[2016,256]{1,0:T(8,128)(2,1)} %get-tuple-element.49), channel_id=1, source_target_pairs={{0,64},{4,68},{8,72},{12,76},{16,80},{20,84},{24,88},{28,92},{32,9... | collective-permute-start | bytes 3096584 | tf_op jit(solution)/shard_map/ppermute | solution.py:588
  84.2 57.3 %copy-start.6 = (s32[4000]{0:T(1024)}, s32[4000]{0:T(1024)S(1)}, u32[]{:S(2)}) copy-start(s32[4000]{0:T(1024)S(1)} %reshape_squeeze.13.refs_2_.index_ref.refs_1_) | copy-start | bytes 48004
  141.5 10.2 %copy-start.11 = (s32[9,1000]{1,0:T(8,128)S(1)}, s32[9,1000]{1,0:T(8,128)}, u32[]{:S(2)}) copy-start(s32[9,1000]{1,0:T(8,128)} %get-tuple-element.39) | copy-start | bytes 108004
  141.6 80.7 %collective-permute-start.6 = (bf16[2016,256]{1,0:T(8,128)(2,1)}, bf16[2016,256]{1,0:T(8,128)(2,1)S(1)}, u32[]{:S(2)}, u32[]{:S(2)}) collective-permute-start(bf16[2016,256]{1,0:T(8,128)(2,1)} %get-tuple-element.50), channel_id=1, source_target_pairs={{0,32},{4,36},{8,40},{12,44},{16,48},{20,52},{24,56},{28,60},{32,0... | collective-permute-start | bytes 3096584 | tf_op jit(solution)/shard_map/ppermute | solution.py:588
  141.7 63.4 %copy-start.8 = (f32[64,256]{1,0:T(8,128)S(1)}, f32[64,256]{1,0:T(8,128)}, u32[]{:S(2)}) copy-start(f32[64,256]{1,0:T(8,128)} %refs_5_.1) | copy-start | bytes 196612
  149.7 107.9 %copy-start.7 = (s32[4000]{0:T(1024)S(1)}, s32[4000]{0:T(1024)}, u32[]{:S(2)}) copy-start(s32[4000]{0:T(1024)} %copy-done.6) | copy-start | bytes 48004
  149.7 78.1 %collective-permute-start.10 = (bf16[2016,256]{1,0:T(8,128)(2,1)}, bf16[2016,256]{1,0:T(8,128)(2,1)S(1)}, u32[]{:S(2)}, u32[]{:S(2)}) collective-permute-start(bf16[2016,256]{1,0:T(8,128)(2,1)} %shard_map.115), channel_id=1, source_target_pairs={{0,32},{4,36},{8,40},{12,44},{16,48},{20,52},{24,56},{28,60},{32,0... | collective-permute-start | bytes 3096584 | tf_op jit(solution)/shard_map/ppermute | solution.py:588
  151.8 38.6 %collective-permute-start = (s32[9,1000]{1,0:T(8,128)S(1)}, s32[9,1000]{1,0:T(8,128)S(1)}, u32[]{:S(2)}, u32[]{:S(2)}) collective-permute-start(s32[9,1000]{1,0:T(8,128)S(1)} %copy-done.11), channel_id=1, source_target_pairs={{0,32},{4,36},{8,40},{12,44},{16,48},{20,52},{24,56},{28,60},{32,0... | collective-permute-start | bytes 108008 | tf_op jit(solution)/shard_map/ppermute | solution.py:588
  191.0 14.0 %collective-permute-start.7 = (f32[64,256]{1,0:T(8,128)S(1)}, f32[64,256]{1,0:T(8,128)S(1)}, u32[]{:S(2)}, u32[]{:S(2)}) collective-permute-start(f32[64,256]{1,0:T(8,128)S(1)} %get-tuple-element.56.refs_0_), channel_id=1, source_target_pairs={{0,32},{4,36},{8,40},{12,44},{16,48},{20,52},{24,56},{28,60},{32,0... | collective-permute-start | bytes 196616 | tf_op jit(solution)/shard_map/ppermute | solution.py:588
  191.3 13.7 %collective-permute-start.8 = (f32[64,256]{1,0:T(8,128)S(1)}, f32[64,256]{1,0:T(8,128)S(1)}, u32[]{:S(2)}, u32[]{:S(2)}) collective-permute-start(f32[64,256]{1,0:T(8,128)S(1)} %get-tuple-element.56.refs_0_), channel_id=1, source_target_pairs={{0,64},{4,68},{8,72},{12,76},{16,80},{20,84},{24,88},{28,92},{32,9... | collective-permute-start | bytes 196616 | tf_op jit(solution)/shard_map/ppermute | solution.py:588
  194.5 10.5 %collective-permute-start.9 = (f32[64,256]{1,0:T(8,128)S(1)}, f32[64,256]{1,0:T(8,128)S(1)}, u32[]{:S(2)}, u32[]{:S(2)}) collective-permute-start(f32[64,256]{1,0:T(8,128)S(1)} %get-tuple-element.56.refs_0_), channel_id=1, source_target_pairs={{0,96},{4,100},{8,104},{12,108},{16,112},{20,116},{24,120},{28,124... | collective-permute-start | bytes 196616 | tf_op jit(solution)/shard_map/ppermute | solution.py:588
  227.7 29.9 %collective-permute-start.11 = (bf16[2016,256]{1,0:T(8,128)(2,1)S(1)}, bf16[2016,256]{1,0:T(8,128)(2,1)S(1)}, u32[]{:S(2)}, u32[]{:S(2)}) collective-permute-start(bf16[2016,256]{1,0:T(8,128)(2,1)S(1)} %get-tuple-element.65), channel_id=1, source_target_pairs={{0,32},{4,36},{8,40},{12,44},{16,48},{20,52},{24,56},{28,60},{32,0... | collective-permute-start | bytes 3096584 | tf_op jit(solution)/shard_map/ppermute | solution.py:588
  233.6 1.3 copy-start
  234.9 43.4 %collective-permute-start.12 = (bf16[2016,256]{1,0:T(8,128)(2,1)S(1)}, bf16[2016,256]{1,0:T(8,128)(2,1)S(1)}, u32[]{:S(2)}, u32[]{:S(2)}) collective-permute-start(bf16[2016,256]{1,0:T(8,128)(2,1)S(1)} %get-tuple-element.66), channel_id=1, source_target_pairs={{0,32},{4,36},{8,40},{12,44},{16,48},{20,52},{24,56},{28,60},{32,0... | collective-permute-start | bytes 3096584 | tf_op jit(solution)/shard_map/ppermute | solution.py:588
  252.8 25.4 %collective-permute-start.13 = (f32[64,256]{1,0:T(8,128)S(1)}, f32[64,256]{1,0:T(8,128)S(1)}, u32[]{:S(2)}, u32[]{:S(2)}) collective-permute-start(f32[64,256]{1,0:T(8,128)S(1)} %shard_map.116.refs_6_), channel_id=1, source_target_pairs={{0,32},{4,36},{8,40},{12,44},{16,48},{20,52},{24,56},{28,60},{32,0... | collective-permute-start | bytes 196616 | tf_op jit(solution)/shard_map/ppermute | solution.py:588
  252.9 25.3 %collective-permute-start.14 = (f32[64,256]{1,0:T(8,128)S(1)}, f32[64,256]{1,0:T(8,128)S(1)}, u32[]{:S(2)}, u32[]{:S(2)}) collective-permute-start(f32[64,256]{1,0:T(8,128)S(1)} %shard_map.116.refs_6_), channel_id=1, source_target_pairs={{0,64},{4,68},{8,72},{12,76},{16,80},{20,84},{24,88},{28,92},{32,9... | collective-permute-start | bytes 196616 | tf_op jit(solution)/shard_map/ppermute | solution.py:588
  255.2 23.0 %collective-permute-start.15 = (f32[64,256]{1,0:T(8,128)S(1)}, f32[64,256]{1,0:T(8,128)S(1)}, u32[]{:S(2)}, u32[]{:S(2)}) collective-permute-start(f32[64,256]{1,0:T(8,128)S(1)} %shard_map.116.refs_6_), channel_id=1, source_target_pairs={{0,96},{4,100},{8,104},{12,108},{16,112},{20,116},{24,120},{28,124... | collective-permute-start | bytes 196616 | tf_op jit(solution)/shard_map/ppermute | solution.py:588

commit v3 on v2

--- a/solution.py
+++ b/solution.py
@@ -122,9 +122,8 @@
             load.start()
             loads.append(load)
         for number, note in enumerate(notes):
-            note[:slots] = dst_ref[number]
-            note[slots : 2 * slots] = rel_ref[number]
-            note[2 * slots :] = jnp.full((1, count), count_ref[number], jnp.int32)
+            note[:slots] = dst_ref[number] + rel_ref[number] * row_count
+            note[slots:] = jnp.full((1, count), count_ref[number], jnp.int32)
         for part in range(parts):
             loads[part].wait()
 
@@ -144,7 +143,7 @@
     return pl.pallas_call(
         body,
         out_shape=[jax.ShapeDtypeStruct((2 * row_count, LANES), jnp.float32)]
-        + [jax.ShapeDtypeStruct((2 * slots + 1, count), jnp.int32)] * rounds
+        + [jax.ShapeDtypeStruct((slots + 1, count), jnp.int32)] * rounds
         + [jax.ShapeDtypeStruct((len(batches) * height, width), jnp.bfloat16)],
         in_specs=[SMEM, SMEM, HBM, VMEM, VMEM],
         out_specs=[HBM] + [VMEM] * (rounds + 1),
@@ -341,7 +340,7 @@
         + [pltpu.VMEM(own[0].shape, jnp.float32)] * len(returned)
         + [pltpu.VMEM((2 * row_count, LANES), jnp.float32)] * 2
         + [pltpu.SemaphoreType.DMA((loads + parts,))],
-        compiler_params=params(50),
+        compiler_params=params(44),
         cost_estimate=cost(60_000_000),
         name="first_total",
     )(live, other_live, source_index, other_index, *own, *returned)
@@ -479,28 +478,32 @@
     return index
 
 
-def relation_kernel(stages, near, finish, *scratch):
-    parts, received = scratch[:-3], scratch[-3]
-    send_sems, recv_sems = scratch[-2:]
+def relation_kernel(near, finish, whole, parts, received, send_sems, recv_sems):
     dom, rep = lax.axis_index("dom"), lax.axis_index("rep")
+    rows = parts.shape[1]
+    core = rep % 2
 
     def device(peer):
         return (flip(dom, peer[0]), flip(rep, peer[1]))
 
+    def mine(which):
+        return pl.ds(pl.multiple_of(which * rows, rows), rows)
+
     barrier = pltpu.get_barrier_semaphore()
-    peers = [peer for stage in stages for peer in stage]
+    peers = [peer for stage in STAGES[:-1] for peer in stage]
     for peer in peers:
         pl.semaphore_signal(
             barrier, inc=1, device_id=device(peer), device_id_type=pl.DeviceIdType.MESH
         )
     pl.semaphore_wait(barrier, len(peers))
-    parts[0][...] = pair_sum([ref[...] for ref in near])
+    whole[...] = pair_sum([ref[...] for ref in near])
     slot = 0
-    for number, stage in enumerate(stages):
+    for number, stage in enumerate(STAGES):
+        source = whole.at[mine(1 - core)] if number == 0 else parts.at[number - 1]
         copies = []
         for peer in stage:
             copy = pltpu.make_async_remote_copy(
-                src_ref=parts[number],
+                src_ref=source,
                 dst_ref=received.at[slot],
                 send_sem=send_sems.at[slot],
                 recv_sem=recv_sems.at[slot],
@@ -512,11 +515,14 @@
             slot += 1
         for copy in copies:
             copy.wait()
-        first = slot - len(stage)
-        total = pair_sum([parts[number][...]] + [received[first + i] for i in range(len(stage))])
-        if number + 1 < len(stages):
-            parts[number + 1][...] = total
-    finish(total)
+        own = whole[mine(core), :] if number == 0 else parts[number - 1]
+        news = [received[slot - len(stage) + i] for i in range(len(stage))]
+        if number + 1 < len(STAGES):
+            parts[number] = pair_sum([own] + news)
+        else:
+            low = jnp.where(core == 0, own, news[0])
+            high = jnp.where(core == 0, news[0], own)
+            finish(jnp.concatenate([low, high], axis=0))
 
 
 def pair_sum(values):
@@ -525,17 +531,28 @@
     return values[0]
 
 
+STAGES = (
+    ((0, 1),),
+    ((0, 2),),
+    ((1, 0), (2, 0), (3, 0)),
+    ((4, 0),),
+    ((0, 1),),
+)
+
+
 def relation_call(body, inputs, outputs, collective_id):
     slots = sum(len(stage) for stage in STAGES)
     shape = inputs[0].shape
+    half_shape = (shape[0] // 2, shape[1])
     return pl.pallas_call(
         body,
         out_shape=[jax.ShapeDtypeStruct(shape, jnp.float32)] * outputs,
         in_specs=[VMEM] * len(inputs),
         out_specs=[VMEM] * outputs,
-        scratch_shapes=[pltpu.VMEM(shape, jnp.float32)] * len(STAGES)
-        + [
-            pltpu.VMEM((slots,) + shape, jnp.float32),
+        scratch_shapes=[
+            pltpu.VMEM(shape, jnp.float32),
+            pltpu.VMEM((len(STAGES) - 1,) + half_shape, jnp.float32),
+            pltpu.VMEM((slots,) + half_shape, jnp.float32),
             pltpu.SemaphoreType.DMA((slots,)),
             pltpu.SemaphoreType.DMA((slots,)),
         ],
@@ -546,19 +563,12 @@
     )(*inputs)
 
 
-STAGES = (
-    ((0, 1), (0, 2), (0, 3)),
-    ((1, 0), (2, 0), (3, 0)),
-    ((4, 0),),
-)
-
-
 def relation_sum(rel_grad):
     def body(own, summed, *scratch):
         def finish(total):
             summed[...] = total
 
-        relation_kernel(STAGES, [own], finish, *scratch)
+        relation_kernel([own], finish, *scratch)
 
     return relation_call(body, [rel_grad], 1, 0)[0]
 
@@ -575,7 +585,7 @@
             new_state[...] = state
             new_rel[...] = rel_ref[...] - rel_rate * total / jnp.sqrt(state)
 
-        relation_kernel(STAGES, near_refs, finish, *refs[count + 4 :])
+        relation_kernel(near_refs, finish, *refs[count + 4 :])
 
     return relation_call(body, [*near, relations, rel_state], 2, 1)
 
@@ -615,10 +625,10 @@
         more = pack(source_index, table, groups[1:], count, width, 54)
         for rows in more:
             arrived.append(from_partner(rows, "dom", swap_bit))
-        other_index = note[:batches].reshape(-1)
-        other_live = note[2 * batches, :1]
+        other_index = (note[:batches] % row_count).reshape(-1)
+        other_live = note[batches, :1]
         kinds = jnp.pad(
-            note[batches : 2 * batches], ((0, 0), (0, padded - count)), constant_values=-1
+            note[:batches] // row_count, ((0, 0), (0, padded - count)), constant_values=-1
         )
         targets = pack(other_index, table, groups, count, width, 50)
         if number:

time: 292 us -> 290 us (level)
  the two profiles are of different devices: /device:TPU:2 before, /device:TPU:1 now
where the time goes in v3:
time: 290 us
  Pallas kernels  157 us (54%)
  waiting for transfers between devices  96.4 us (33%)
  starting transfers between devices  26.2 us (9%)
  local copies, waits for them, and re-layouts  8.52 us (3%)
    ppermute x16, waiting for transfers between devices, from_peer(): lax.ppermute(shard, axis, [(i, i ^ bits) for i in range(lax.axis_size(axi...  96.4 us
    pallas_call x2, Pallas kernels, relation_call(): pl.pallas_call(body, out_shape=[jax.ShapeDtypeStruct(shape, jnp.float32)]...  47.6 us
    pallas_call x4, Pallas kernels, pack(): pl.pallas_call(body, out_shape=[jax.ShapeDtypeStruct((len(group) * height...  34.6 us
    pallas_call x2, Pallas kernels, first_total(): pl.pallas_call(body, out_shape=jax.ShapeDtypeStruct((2 * row_count, LANES...  29.4 us
    pallas_call x2, Pallas kernels, finish(): pl.pallas_call(body, out_shape=[jax.ShapeDtypeStruct(out_shape, jnp.float...  27.3 us
    ppermute x16, starting transfers between devices, from_peer(): lax.ppermute(shard, axis, [(i, i ^ bits) for i in range(lax.axis_size(axi...  26.2 us
    pallas_call x4, Pallas kernels, run_group(): pl.pallas_call(functools.partial(batch_kernel, group, count), out_shape=[...  9.56 us
    pallas_call x1, Pallas kernels, pack_first(): pl.pallas_call(body, out_shape=[jax.ShapeDtypeStruct((2 * row_count, LANE...  8.91 us
  transfers between devices with their start and end apart: 16, of which 6 were waited for; matrix products, arithmetic and copies ran while one was open for 1% of the time, Pallas kernels for 42%

profile of v3, /device:TPU:1, one launch (start us, length us, event | category | flops | bytes accessed | tf_op | source)
XLA Modules:
  0.0 289.7 jit_solution(10681221420878316735)
XLA Ops:
  0.6 0.7 fusion.2
  1.4 0.7 reshape_squeeze.14.index_ref.refs_1_
  2.1 8.9 %pack_first.1 = (f32[16384,128]{1,0:T(8,128)}, s32[5,1000]{1,0:T(8,128)}, s32[5,1000]{1,0:T(8,128)}, bf16[2016,256]{1,0:T(8,128)(2,1)}) custom-call(s32[4000]{0:T(1024)} %reshape_squeeze.14.index_ref.refs_1_, s32[2]{0:T(128)} %bitcast.12, f32[8192,256]{1,0:T(8,128)} %table_hbm.1, s32[2,4,1000]{2,1,0:T(4,128)} %bitcast.10, s32[2,4,1000]{2,1,0:T(4,128)} %bitcast.11), custom_call_target="tpu_custom_call" | custom-call | bytes 25000000 | tf_op jit(solution)/shard_map/pack_first/pallas_call | solution.py:143
  11.0 4.5 %collective-permute-start.2 = (bf16[2016,256]{1,0:T(8,128)(2,1)}, bf16[2016,256]{1,0:T(8,128)(2,1)S(1)}, u32[]{:S(2)}, u32[]{:S(2)}) collective-permute-start(bf16[2016,256]{1,0:T(8,128)(2,1)} %get-tuple-element.41), channel_id=1, source_target_pairs={{0,64},{4,68},{8,72},{12,76},{16,80},{20,84},{24,88},{28,92},{32,9... | collective-permute-start | bytes 3096584 | tf_op jit(solution)/shard_map/ppermute | solution.py:598
  15.5 8.0 %shard_map.112 = bf16[2016,256]{1,0:T(8,128)(2,1)} custom-call(s32[4000]{0:T(1024)} %reshape_squeeze.14.index_ref.refs_1_, f32[16384,128]{1,0:T(8,128)} %get-tuple-element.42.table_hbm.refs_5_), custom_call_target="tpu_custom_call" | custom-call | bytes 30000000 | tf_op jit(solution)/shard_map/pallas_call | solution.py:173
  23.5 0.1 collective-permute-start.3
  23.6 2.9 %collective-permute-start.1 = (s32[5,1000]{1,0:T(8,128)S(1)}, s32[5,1000]{1,0:T(8,128)S(1)}, u32[]{:S(2)}, u32[]{:S(2)}) collective-permute-start(s32[5,1000]{1,0:T(8,128)S(1)} %copy-done.12), channel_id=1, source_target_pairs={{0,64},{4,68},{8,72},{12,76},{16,80},{20,84},{24,88},{28,92},{32,9... | collective-permute-start | bytes 60008 | tf_op jit(solution)/shard_map/ppermute | solution.py:598
  26.6 34.4 %collective-permute-done.1 = s32[5,1000]{1,0:T(8,128)S(1)} collective-permute-done((s32[5,1000]{1,0:T(8,128)S(1)}, s32[5,1000]{1,0:T(8,128)S(1)}, u32[]{:S(2)}, u32[]{:S(2)}) %collective-permute-start.1) | collective-permute-done | bytes 20032 | tf_op jit(solution)/shard_map/ppermute | solution.py:598
  61.1 0.1 reshape.21.index_ref.source_ref
  61.2 9.3 %shard_map.111 = (bf16[2016,256]{1,0:T(8,128)(2,1)S(1)}, bf16[2016,256]{1,0:T(8,128)(2,1)S(1)}) custom-call(s32[4000]{0:T(1024)S(1)} %reshape.21.index_ref.source_ref, f32[16384,128]{1,0:T(8,128)} %get-tuple-element.42.table_hbm.refs_5_), custom_call_target="tpu_custom_call" | custom-call | bytes 30000000 | tf_op jit(solution)/shard_map/pallas_call | solution.py:173
  70.5 0.5 slice.52
  71.0 1.0 copy-done.2
  72.0 1.2 copy-done.3
  73.2 4.0 %batch_terms.4 = (bf16[2016,256]{1,0:T(8,128)(2,1)}, f32[4032,128]{1,0:T(8,128)S(1)}, f32[64,256]{1,0:T(8,128)S(1)}) custom-call(s32[1]{0:T(128)} %bitcast.6.live_ref, s32[2,1024]{1,0:T(2,128)S(1)} %get-tuple-element.83.kind_ref, bf16[2016,256]{1,0:T(8,128)(2,1)S(1)} %copy-done.3, bf16[2016,256]{1,0:T(8,128)(2,1)S(1)} %get-tuple-element.43.target_ref, ...), custom_call_target="tpu_custom_call" | custom-call | bytes 15000000 | tf_op jit(solution)/shard_map/batch_terms/pallas_call | solution.py:271
  77.3 2.7 collective-permute-start.4
  80.0 1.6 batch_terms.5
  81.6 1.4 copy-done
  82.9 0.3 collective-permute-start.5
  83.2 0.1 reshape_squeeze.13.refs_2_.index_ref.refs_1_
  83.3 0.6 fusion.3
  83.9 17.0 %collective-permute-done.4.refs_2_ = bf16[2016,256]{1,0:T(8,128)(2,1)} collective-permute-done((bf16[2016,256]{1,0:T(8,128)(2,1)}, bf16[2016,256]{1,0:T(8,128)(2,1)}, u32[]{:S(2)}, u32[]{:S(2)}) %collective-permute-start.4) | collective-permute-done | bytes 1032224 | tf_op jit(solution)/shard_map/ppermute | solution.py:598
  100.9 1.6 copy-done.1
  102.5 14.0 %first_total.2.refs_3_ = f32[16384,128]{1,0:T(8,128)} custom-call(s32[1]{0:T(128)} %bitcast.6.live_ref, s32[1]{0:T(128)} %bitcast.5.other_ref.refs_0_, s32[4000]{0:T(1024)S(1)} %reshape.21.index_ref.source_ref, s32[4000]{0:T(1024)S(1)} %copy-done.5, f32[4032,128]{1,0:T(8,128)S(1)} %get-tuple-element.44.refs_0_, f32[4032,128]{1,0:T(8,128)S(1)} %copy-done.1, ...), custom_call_target="tpu_custom_call" | custom-call | bytes 60000000 | tf_op jit(solution)/shard_map/first_total/pallas_call | solution.py:334
  116.5 6.6 %collective-permute-done.5.refs_4_ = bf16[2016,256]{1,0:T(8,128)(2,1)S(1)} collective-permute-done((bf16[2016,256]{1,0:T(8,128)(2,1)}, bf16[2016,256]{1,0:T(8,128)(2,1)S(1)}, u32[]{:S(2)}, u32[]{:S(2)}) %collective-permute-start.5) | collective-permute-done | bytes 1032224 | tf_op jit(solution)/shard_map/ppermute | solution.py:598
  123.0 14.8 %finish_next.1 = (f32[16384,128]{1,0:T(8,128)}, f32[64,128]{1,0:T(8,128)S(1)}, bf16[2016,256]{1,0:T(8,128)(2,1)}) custom-call(s32[1]{0:T(128)} %bitcast.5.other_ref.refs_0_, s32[4000]{0:T(1024)S(1)} %copy-done.5, s32[4000]{0:T(1024)S(1)} %reshape_squeeze.13.refs_2_.index_ref.refs_1_, f32[16384,128]{1,0:T(8,128)} %first_total.2.refs_3_, ...), custom_call_target="tpu_custom_call" | custom-call | bytes 50000000 | tf_op jit(solution)/shard_map/finish_next/pallas_call | solution.py:441
  137.8 0.1 collective-permute-start.6
  138.0 8.0 %shard_map.115 = bf16[2016,256]{1,0:T(8,128)(2,1)} custom-call(s32[4000]{0:T(1024)} %copy-done.6, f32[16384,128]{1,0:T(8,128)} %get-tuple-element.52.table_hbm.refs_4_), custom_call_target="tpu_custom_call" | custom-call | bytes 30000000 | tf_op jit(solution)/shard_map/pallas_call | solution.py:173
  146.0 1.5 collective-permute-start.10
  147.5 0.1 collective-permute-start
  147.6 30.7 %collective-permute-done = s32[5,1000]{1,0:T(8,128)S(1)} collective-permute-done((s32[5,1000]{1,0:T(8,128)S(1)}, s32[5,1000]{1,0:T(8,128)S(1)}, u32[]{:S(2)}, u32[]{:S(2)}) %collective-permute-start) | collective-permute-done | bytes 20032 | tf_op jit(solution)/shard_map/ppermute | solution.py:598
  178.4 0.1 reshape.20.index_ref.source_ref
  178.5 0.5 slice.50
  179.0 5.1 %collective-permute-start.8 = (f32[64,256]{1,0:T(8,128)S(1)}, f32[64,256]{1,0:T(8,128)S(1)}, u32[]{:S(2)}, u32[]{:S(2)}) collective-permute-start(f32[64,256]{1,0:T(8,128)S(1)} %get-tuple-element.56.refs_0_), channel_id=1, source_target_pairs={{0,64},{4,68},{8,72},{12,76},{16,80},{20,84},{24,88},{28,92},{32,9... | collective-permute-start | bytes 196616 | tf_op jit(solution)/shard_map/ppermute | solution.py:598
  184.1 0.3 collective-permute-start.9
  184.3 9.3 %shard_map.113 = (bf16[2016,256]{1,0:T(8,128)(2,1)S(1)}, bf16[2016,256]{1,0:T(8,128)(2,1)S(1)}) custom-call(s32[4000]{0:T(1024)S(1)} %reshape.20.index_ref.source_ref, f32[16384,128]{1,0:T(8,128)} %get-tuple-element.52.table_hbm.refs_4_), custom_call_target="tpu_custom_call" | custom-call | bytes 30000000 | tf_op jit(solution)/shard_map/pallas_call | solution.py:173
  193.7 28.4 %shard_map.114 = (f32[64,256]{1,0:T(8,128)S(1)}, f32[64,256]{1,0:T(8,128)S(1)}) custom-call(f32[64,256]{1,0:T(8,128)S(1)} %get-tuple-element.56.refs_0_, f32[64,256]{1,0:T(8,128)S(1)} %collective-permute-done.7.refs_1_, f32[64,256]{1,0:T(8,128)S(1)} %collective-permute-done.8.refs_2_, f32[64,256]{1,0:T(8,128)S(1)} %collective-permute-done.9.refs_3_, ...), custom_call_target="tpu_custom_call" | custom-call | bytes 20000000 | tf_op jit(solution)/shard_map/pallas_call | solution.py:547
  222.1 3.0 %batch_terms.6 = (bf16[2016,256]{1,0:T(8,128)(2,1)S(1)}, f32[4032,128]{1,0:T(8,128)S(1)}, f32[64,256]{1,0:T(8,128)S(1)}) custom-call(s32[1]{0:T(128)} %bitcast.4.live_ref, s32[2,1024]{1,0:T(2,128)S(1)} %get-tuple-element.81.kind_ref, bf16[2016,256]{1,0:T(8,128)(2,1)S(1)} %collective-permute-done.6.source_ref, ...), custom_call_target="tpu_custom_call" | custom-call | bytes 15000000 | tf_op jit(solution)/shard_map/batch_terms/pallas_call | solution.py:271
  225.1 2.2 collective-permute-start.11
  227.4 0.9 batch_terms.7
  228.2 2.5 collective-permute-start.12
  230.7 19.2 %shard_map.116.refs_6_ = f32[64,256]{1,0:T(8,128)S(1)} custom-call(f32[64,256]{1,0:T(8,128)S(1)} %get-tuple-element.68.own), custom_call_target="tpu_custom_call" | custom-call | bytes 20000000 | tf_op jit(solution)/shard_map/pallas_call | solution.py:547
  249.9 0.1 collective-permute-start.13
  250.0 2.2 collective-permute-start.14
  252.3 1.6 collective-permute-start.15
  253.9 15.5 %first_total.3.refs_2_ = f32[16384,128]{1,0:T(8,128)} custom-call(s32[1]{0:T(128)} %bitcast.4.live_ref, s32[1]{0:T(128)} %bitcast.other_ref.refs_0_, s32[4000]{0:T(1024)S(1)} %reshape.20.index_ref.source_ref, s32[4000]{0:T(1024)S(1)} %copy-done.7, f32[4032,128]{1,0:T(8,128)S(1)} %get-tuple-element.61.refs_0_, f32[4032,128]{1,0:T(8,128)S(1)} %get-tuple-element.64.refs_1_, ...), custom_call_target="tpu_custom_call" | custom-call | bytes 60000000 | tf_op jit(solution)/shard_map/first_total/pallas_call | solution.py:334
  269.3 3.5 %collective-permute-done.13.refs_7_ = f32[64,256]{1,0:T(8,128)S(1)} collective-permute-done((f32[64,256]{1,0:T(8,128)S(1)}, f32[64,256]{1,0:T(8,128)S(1)}, u32[]{:S(2)}, u32[]{:S(2)}) %collective-permute-start.13) | collective-permute-done | bytes 65568 | tf_op jit(solution)/shard_map/ppermute | solution.py:598
  272.8 4.2 %collective-permute-done.14.refs_8_ = f32[64,256]{1,0:T(8,128)S(1)} collective-permute-done((f32[64,256]{1,0:T(8,128)S(1)}, f32[64,256]{1,0:T(8,128)S(1)}, u32[]{:S(2)}, u32[]{:S(2)}) %collective-permute-start.14) | collective-permute-done | bytes 65568 | tf_op jit(solution)/shard_map/ppermute | solution.py:598
  277.0 12.5 %finish_last.1 = (f32[8192,256]{1,0:T(8,128)}, f32[64,128]{1,0:T(8,128)}, f32[64,256]{1,0:T(8,128)}, f32[64,256]{1,0:T(8,128)}) custom-call(s32[1]{0:T(128)} %bitcast.other_ref.refs_0_, s32[4000]{0:T(1024)S(1)} %copy-done.7, f32[16384,128]{1,0:T(8,128)} %first_total.3.refs_2_, bf16[2016,256]{1,0:T(8,128)(2,1)S(1)} %collective-permute-done.12.refs_3_, ...), custom_call_target="tpu_custom_call" | custom-call | bytes 50000000 | tf_op jit(solution)/shard_map/finish_last/pallas_call | solution.py:441
  (40 shorter events, 0.2 us)
Async XLA Ops:
  11.0 12.7 %copy-start.12 = (s32[5,1000]{1,0:T(8,128)S(1)}, s32[5,1000]{1,0:T(8,128)}, u32[]{:S(2)}) copy-start(s32[5,1000]{1,0:T(8,128)} %get-tuple-element.40) | copy-start | bytes 60004
  11.0 60.0 %collective-permute-start.2 = (bf16[2016,256]{1,0:T(8,128)(2,1)}, bf16[2016,256]{1,0:T(8,128)(2,1)S(1)}, u32[]{:S(2)}, u32[]{:S(2)}) collective-permute-start(bf16[2016,256]{1,0:T(8,128)(2,1)} %get-tuple-element.41), channel_id=1, source_target_pairs={{0,64},{4,68},{8,72},{12,76},{16,80},{20,84},{24,88},{28,92},{32,9... | collective-permute-start | bytes 3096584 | tf_op jit(solution)/shard_map/ppermute | solution.py:598
  15.5 56.5 %copy-start.4 = (f32[64,256]{1,0:T(8,128)S(1)}, f32[64,256]{1,0:T(8,128)}, u32[]{:S(2)}) copy-start(f32[64,256]{1,0:T(8,128)} %refs_4_.1) | copy-start | bytes 196612
  23.5 59.8 %copy-start.10 = (s32[1,1,2]{2,1,0:T(1,128)S(1)}, s32[1,1,2]{2,1,0:T(1,128)}, u32[]{:S(2)}) copy-start(s32[1,1,2]{2,1,0:T(1,128)} %param.15) | copy-start | bytes 28
  23.5 77.4 %copy-start.5 = (s32[4000]{0:T(1024)S(1)}, s32[4000]{0:T(1024)}, u32[]{:S(2)}) copy-start(s32[4000]{0:T(1024)} %reshape_squeeze.14.index_ref.refs_1_) | copy-start | bytes 48004
  23.5 56.4 %collective-permute-start.3 = (bf16[2016,256]{1,0:T(8,128)(2,1)}, bf16[2016,256]{1,0:T(8,128)(2,1)S(1)}, u32[]{:S(2)}, u32[]{:S(2)}) collective-permute-start(bf16[2016,256]{1,0:T(8,128)(2,1)} %shard_map.112), channel_id=1, source_target_pairs={{0,64},{4,68},{8,72},{12,76},{16,80},{20,84},{24,88},{28,92},{32,9... | collective-permute-start | bytes 3096584 | tf_op jit(solution)/shard_map/ppermute | solution.py:598
  23.6 37.4 %collective-permute-start.1 = (s32[5,1000]{1,0:T(8,128)S(1)}, s32[5,1000]{1,0:T(8,128)S(1)}, u32[]{:S(2)}, u32[]{:S(2)}) collective-permute-start(s32[5,1000]{1,0:T(8,128)S(1)} %copy-done.12), channel_id=1, source_target_pairs={{0,64},{4,68},{8,72},{12,76},{16,80},{20,84},{24,88},{28,92},{32,9... | collective-permute-start | bytes 60008 | tf_op jit(solution)/shard_map/ppermute | solution.py:598
  71.0 1.0 copy-start.2
  72.0 1.2 copy-start.3
  77.3 45.8 %copy-start.9 = (f32[8192]{0:T(1024)S(1)}, f32[8192]{0:T(1024)}, u32[]{:S(2)}) copy-start(f32[8192]{0:T(1024)} %param.9) | copy-start | bytes 98308
  77.3 23.6 %collective-permute-start.4 = (bf16[2016,256]{1,0:T(8,128)(2,1)}, bf16[2016,256]{1,0:T(8,128)(2,1)}, u32[]{:S(2)}, u32[]{:S(2)}) collective-permute-start(bf16[2016,256]{1,0:T(8,128)(2,1)} %get-tuple-element.48), channel_id=1, source_target_pairs={{0,64},{4,68},{8,72},{12,76},{16,80},{20,84},{24,88},{28,92},{32,9... | collective-permute-start | bytes 3096584 | tf_op jit(solution)/shard_map/ppermute | solution.py:598
  81.6 1.4 copy-start
  82.9 40.1 %collective-permute-start.5 = (bf16[2016,256]{1,0:T(8,128)(2,1)}, bf16[2016,256]{1,0:T(8,128)(2,1)S(1)}, u32[]{:S(2)}, u32[]{:S(2)}) collective-permute-start(bf16[2016,256]{1,0:T(8,128)(2,1)} %get-tuple-element.49), channel_id=1, source_target_pairs={{0,64},{4,68},{8,72},{12,76},{16,80},{20,84},{24,88},{28,92},{32,9... | collective-permute-start | bytes 3096584 | tf_op jit(solution)/shard_map/ppermute | solution.py:598
  83.3 54.5 %copy-start.6 = (s32[4000]{0:T(1024)}, s32[4000]{0:T(1024)S(1)}, u32[]{:S(2)}) copy-start(s32[4000]{0:T(1024)S(1)} %reshape_squeeze.13.refs_2_.index_ref.refs_1_) | copy-start | bytes 48004
  100.9 1.6 copy-start.1
  137.8 9.6 %copy-start.11 = (s32[5,1000]{1,0:T(8,128)S(1)}, s32[5,1000]{1,0:T(8,128)}, u32[]{:S(2)}) copy-start(s32[5,1000]{1,0:T(8,128)} %get-tuple-element.39) | copy-start | bytes 60004
  137.8 84.2 %collective-permute-start.6 = (bf16[2016,256]{1,0:T(8,128)(2,1)}, bf16[2016,256]{1,0:T(8,128)(2,1)S(1)}, u32[]{:S(2)}, u32[]{:S(2)}) collective-permute-start(bf16[2016,256]{1,0:T(8,128)(2,1)} %get-tuple-element.50), channel_id=1, source_target_pairs={{0,32},{4,36},{8,40},{12,44},{16,48},{20,52},{24,56},{28,60},{32,0... | collective-permute-start | bytes 3096584 | tf_op jit(solution)/shard_map/ppermute | solution.py:598
  137.9 55.7 %copy-start.8 = (f32[64,256]{1,0:T(8,128)S(1)}, f32[64,256]{1,0:T(8,128)}, u32[]{:S(2)}) copy-start(f32[64,256]{1,0:T(8,128)} %refs_5_.1) | copy-start | bytes 196612
  145.9 107.9 %copy-start.7 = (s32[4000]{0:T(1024)S(1)}, s32[4000]{0:T(1024)}, u32[]{:S(2)}) copy-start(s32[4000]{0:T(1024)} %copy-done.6) | copy-start | bytes 48004
  146.0 81.4 %collective-permute-start.10 = (bf16[2016,256]{1,0:T(8,128)(2,1)}, bf16[2016,256]{1,0:T(8,128)(2,1)S(1)}, u32[]{:S(2)}, u32[]{:S(2)}) collective-permute-start(bf16[2016,256]{1,0:T(8,128)(2,1)} %shard_map.115), channel_id=1, source_target_pairs={{0,32},{4,36},{8,40},{12,44},{16,48},{20,52},{24,56},{28,60},{32,0... | collective-permute-start | bytes 3096584 | tf_op jit(solution)/shard_map/ppermute | solution.py:598
  147.5 30.8 %collective-permute-start = (s32[5,1000]{1,0:T(8,128)S(1)}, s32[5,1000]{1,0:T(8,128)S(1)}, u32[]{:S(2)}, u32[]{:S(2)}) collective-permute-start(s32[5,1000]{1,0:T(8,128)S(1)} %copy-done.11), channel_id=1, source_target_pairs={{0,32},{4,36},{8,40},{12,44},{16,48},{20,52},{24,56},{28,60},{32,0... | collective-permute-start | bytes 60008 | tf_op jit(solution)/shard_map/ppermute | solution.py:598
  179.0 14.7 %collective-permute-start.7 = (f32[64,256]{1,0:T(8,128)S(1)}, f32[64,256]{1,0:T(8,128)S(1)}, u32[]{:S(2)}, u32[]{:S(2)}) collective-permute-start(f32[64,256]{1,0:T(8,128)S(1)} %get-tuple-element.56.refs_0_), channel_id=1, source_target_pairs={{0,32},{4,36},{8,40},{12,44},{16,48},{20,52},{24,56},{28,60},{32,0... | collective-permute-start | bytes 196616 | tf_op jit(solution)/shard_map/ppermute | solution.py:598
  179.0 14.7 %collective-permute-start.8 = (f32[64,256]{1,0:T(8,128)S(1)}, f32[64,256]{1,0:T(8,128)S(1)}, u32[]{:S(2)}, u32[]{:S(2)}) collective-permute-start(f32[64,256]{1,0:T(8,128)S(1)} %get-tuple-element.56.refs_0_), channel_id=1, source_target_pairs={{0,64},{4,68},{8,72},{12,76},{16,80},{20,84},{24,88},{28,92},{32,9... | collective-permute-start | bytes 196616 | tf_op jit(solution)/shard_map/ppermute | solution.py:598
  184.1 9.6 %collective-permute-start.9 = (f32[64,256]{1,0:T(8,128)S(1)}, f32[64,256]{1,0:T(8,128)S(1)}, u32[]{:S(2)}, u32[]{:S(2)}) collective-permute-start(f32[64,256]{1,0:T(8,128)S(1)} %get-tuple-element.56.refs_0_), channel_id=1, source_target_pairs={{0,96},{4,100},{8,104},{12,108},{16,112},{20,116},{24,120},{28,124... | collective-permute-start | bytes 196616 | tf_op jit(solution)/shard_map/ppermute | solution.py:598
  225.1 28.7 %collective-permute-start.11 = (bf16[2016,256]{1,0:T(8,128)(2,1)S(1)}, bf16[2016,256]{1,0:T(8,128)(2,1)S(1)}, u32[]{:S(2)}, u32[]{:S(2)}) collective-permute-start(bf16[2016,256]{1,0:T(8,128)(2,1)S(1)} %get-tuple-element.65), channel_id=1, source_target_pairs={{0,32},{4,36},{8,40},{12,44},{16,48},{20,52},{24,56},{28,60},{32,0... | collective-permute-start | bytes 3096584 | tf_op jit(solution)/shard_map/ppermute | solution.py:598
  228.2 48.8 %collective-permute-start.12 = (bf16[2016,256]{1,0:T(8,128)(2,1)S(1)}, bf16[2016,256]{1,0:T(8,128)(2,1)S(1)}, u32[]{:S(2)}, u32[]{:S(2)}) collective-permute-start(bf16[2016,256]{1,0:T(8,128)(2,1)S(1)} %get-tuple-element.66), channel_id=1, source_target_pairs={{0,32},{4,36},{8,40},{12,44},{16,48},{20,52},{24,56},{28,60},{32,0... | collective-permute-start | bytes 3096584 | tf_op jit(solution)/shard_map/ppermute | solution.py:598
  249.9 22.9 %collective-permute-start.13 = (f32[64,256]{1,0:T(8,128)S(1)}, f32[64,256]{1,0:T(8,128)S(1)}, u32[]{:S(2)}, u32[]{:S(2)}) collective-permute-start(f32[64,256]{1,0:T(8,128)S(1)} %shard_map.116.refs_6_), channel_id=1, source_target_pairs={{0,32},{4,36},{8,40},{12,44},{16,48},{20,52},{24,56},{28,60},{32,0... | collective-permute-start | bytes 196616 | tf_op jit(solution)/shard_map/ppermute | solution.py:598
  250.0 27.0 %collective-permute-start.14 = (f32[64,256]{1,0:T(8,128)S(1)}, f32[64,256]{1,0:T(8,128)S(1)}, u32[]{:S(2)}, u32[]{:S(2)}) collective-permute-start(f32[64,256]{1,0:T(8,128)S(1)} %shard_map.116.refs_6_), channel_id=1, source_target_pairs={{0,64},{4,68},{8,72},{12,76},{16,80},{20,84},{24,88},{28,92},{32,9... | collective-permute-start | bytes 196616 | tf_op jit(solution)/shard_map/ppermute | solution.py:598
  252.3 24.8 %collective-permute-start.15 = (f32[64,256]{1,0:T(8,128)S(1)}, f32[64,256]{1,0:T(8,128)S(1)}, u32[]{:S(2)}, u32[]{:S(2)}) collective-permute-start(f32[64,256]{1,0:T(8,128)S(1)} %shard_map.116.refs_6_), channel_id=1, source_target_pairs={{0,96},{4,100},{8,104},{12,108},{16,112},{20,116},{24,120},{28,124... | collective-permute-start | bytes 196616 | tf_op jit(solution)/shard_map/ppermute | solution.py:598

commit v4 on v3

--- a/solution.py
+++ b/solution.py
@@ -347,7 +347,7 @@
 
 
 def finish(
-    count, groups, live, source_index, total, returned, first, table, state, width, near, relations, rel_state, next_index, next_batches
+    count, groups, live, source_index, total, returned, first, table, state, width, next_index, next_batches
 ):
     row_count = table.shape[0] // 2
     height = returned[0].shape[0]
@@ -369,10 +369,7 @@
         (total_hbm,) = take(1)
         back_refs = take(len(returned))
         table_hbm, state_ref = take(2)
-        near_refs = take(len(near))
-        rel_refs = take(2 if last else 0)
         out_hbm, state_out = take(2)
-        new_rel_refs = take(2 if last else 0)
         next_outs = take(0 if last else 1)
         total_v, other_v, third_v, table_v, state_t, mean_t, sems = take(7)
         rows = take(len(returned))
@@ -385,11 +382,6 @@
         third_v[...] = jnp.zeros_like(third_v)
         for ref, long in zip(back_refs, rows):
             spread(ref, long)
-        if last:
-            rel_total = pair_sum([ref[...] for ref in near_refs])
-            rel_new = rel_refs[1][...] + rel_total * rel_total
-            new_rel_refs[1][...] = rel_new
-            new_rel_refs[0][...] = rel_refs[0][...] - rel_rate * rel_total / jnp.sqrt(rel_new)
         spare = jnp.zeros((LANES - tiles, LANES), jnp.float32)
         state_t[...] = jnp.concatenate([state_ref[...], spare], axis=0).T
         mean_t[...] = jnp.zeros_like(mean_t)
@@ -437,22 +429,20 @@
             save.wait()
 
     out_shape = (row_count, width) if last else table.shape
-    rel_shape = jax.ShapeDtypeStruct(relations.shape, jnp.float32)
     return pl.pallas_call(
         body,
         out_shape=[
             jax.ShapeDtypeStruct(out_shape, jnp.float32),
             jax.ShapeDtypeStruct((tiles, LANES), jnp.float32),
         ]
-        + [rel_shape] * (2 * last)
         + [jax.ShapeDtypeStruct((len(next_batches) * round_up(count, 16), width), jnp.bfloat16)]
         * (not last),
         in_specs=[SMEM] * len(indices)
         + [ANY]
         + [VMEM] * len(returned)
         + [HBM]
-        + [VMEM] * (1 + len(near) + 2 * last),
-        out_specs=[HBM] + [VMEM] * (1 + 2 * last + (not last)),
+        + [VMEM],
+        out_specs=[HBM] + [VMEM] * (1 + (not last)),
         scratch_shapes=[
             pltpu.VMEM(table.shape, jnp.float32),
             pltpu.VMEM(table.shape, jnp.float32),
@@ -467,7 +457,7 @@
         compiler_params=params(50),
         cost_estimate=cost(50_000_000),
         name="finish_last" if last else "finish_next",
-    )(*indices, total, *returned, table, state, *near, *((relations, rel_state) if last else ()))
+    )(*indices, total, *returned, table, state)
 
 
 def flip(index, bits):
@@ -658,7 +648,7 @@
         total = first_total(
             count, groups, row_count, other_live, live, other_index, source_index, own, returned[:early]
         )
-        table, state, *more = finish(
+        table, state, *sent = finish(
             count,
             groups,
             live,
@@ -669,16 +659,12 @@
             table,
             state,
             width,
-            near if last else (),
-            relations,
-            rel_state,
             None if last else sources[number + 1],
             () if last else groups[0],
         )
-        if last:
-            relations, rel_state = more
-        else:
-            sent = more
+    rel_total = pair_sum(near)
+    rel_state = rel_state + rel_total * rel_total
+    relations = relations - rel_rate * rel_total / jnp.sqrt(rel_state)
     return (table, state.reshape(row_count), relations, rel_state)
 
 

time: 290 us -> 310 us (1.069)
  the two profiles are of different devices: /device:TPU:1 before, /device:TPU:4 now
where the time goes in v4:
time: 310 us
  Pallas kernels  157 us (51%)
  waiting for transfers between devices  112 us (36%)
  starting transfers between devices  30.4 us (10%)
  local copies, waits for them, and re-layouts  8.45 us (3%)
    ppermute x16, waiting for transfers between devices, from_peer(): lax.ppermute(shard, axis, [(i, i ^ bits) for i in range(lax.axis_size(axi...  112 us
    pallas_call x2, Pallas kernels, first_total(): pl.pallas_call(body, out_shape=jax.ShapeDtypeStruct((2 * row_count, LANES...  35.9 us
    pallas_call x4, Pallas kernels, pack(): pl.pallas_call(body, out_shape=[jax.ShapeDtypeStruct((len(group) * height...  34.6 us
    pallas_call x2, Pallas kernels, relation_call(): pl.pallas_call(body, out_shape=[jax.ShapeDtypeStruct(shape, jnp.float32)]...  31.4 us
    ppermute x16, starting transfers between devices, from_peer(): lax.ppermute(shard, axis, [(i, i ^ bits) for i in range(lax.axis_size(axi...  30.4 us
    pallas_call x2, Pallas kernels, finish(): pl.pallas_call(body, out_shape=[jax.ShapeDtypeStruct(out_shape, jnp.float...  27.2 us
    pallas_call x4, Pallas kernels, run_group(): pl.pallas_call(functools.partial(batch_kernel, group, count), out_shape=[...  19 us
    pallas_call x1, Pallas kernels, pack_first(): pl.pallas_call(body, out_shape=[jax.ShapeDtypeStruct((2 * row_count, LANE...  8.92 us
  transfers between devices with their start and end apart: 16, of which 6 were waited for; matrix products, arithmetic and copies ran while one was open for 1% of the time, Pallas kernels for 39%

profile of v4, /device:TPU:4, one launch (start us, length us, event | category | flops | bytes accessed | tf_op | source)
XLA Modules:
  0.0 309.7 jit_solution(14698824052585194320)
XLA Ops:
  0.6 0.7 fusion.2
  1.4 0.7 reshape_squeeze.14.index_ref.refs_1_
  2.1 8.9 %pack_first.1 = (f32[16384,128]{1,0:T(8,128)}, s32[5,1000]{1,0:T(8,128)}, s32[5,1000]{1,0:T(8,128)}, bf16[2016,256]{1,0:T(8,128)(2,1)}) custom-call(s32[4000]{0:T(1024)} %reshape_squeeze.14.index_ref.refs_1_, s32[2]{0:T(128)} %bitcast.12, f32[8192,256]{1,0:T(8,128)} %table_hbm.1, s32[2,4,1000]{2,1,0:T(4,128)} %bitcast.10, s32[2,4,1000]{2,1,0:T(4,128)} %bitcast.11), custom_call_target="tpu_custom_call" | custom-call | bytes 25000000 | tf_op jit(solution)/shard_map/pack_first/pallas_call | solution.py:143
  11.0 4.0 %collective-permute-start.2 = (bf16[2016,256]{1,0:T(8,128)(2,1)}, bf16[2016,256]{1,0:T(8,128)(2,1)S(1)}, u32[]{:S(2)}, u32[]{:S(2)}) collective-permute-start(bf16[2016,256]{1,0:T(8,128)(2,1)} %get-tuple-element.39), channel_id=1, source_target_pairs={{0,64},{4,68},{8,72},{12,76},{16,80},{20,84},{24,88},{28,92},{32,9... | collective-permute-start | bytes 3096584 | tf_op jit(solution)/shard_map/ppermute | solution.py:588
  15.0 8.0 %shard_map.112 = bf16[2016,256]{1,0:T(8,128)(2,1)} custom-call(s32[4000]{0:T(1024)} %reshape_squeeze.14.index_ref.refs_1_, f32[16384,128]{1,0:T(8,128)} %get-tuple-element.40.table_hbm.refs_5_), custom_call_target="tpu_custom_call" | custom-call | bytes 30000000 | tf_op jit(solution)/shard_map/pallas_call | solution.py:173
  23.0 0.1 collective-permute-start.3
  23.1 3.5 %collective-permute-start.1 = (s32[5,1000]{1,0:T(8,128)S(1)}, s32[5,1000]{1,0:T(8,128)S(1)}, u32[]{:S(2)}, u32[]{:S(2)}) collective-permute-start(s32[5,1000]{1,0:T(8,128)S(1)} %copy-done.12), channel_id=1, source_target_pairs={{0,64},{4,68},{8,72},{12,76},{16,80},{20,84},{24,88},{28,92},{32,9... | collective-permute-start | bytes 60008 | tf_op jit(solution)/shard_map/ppermute | solution.py:588
  26.6 34.2 %collective-permute-done.1 = s32[5,1000]{1,0:T(8,128)S(1)} collective-permute-done((s32[5,1000]{1,0:T(8,128)S(1)}, s32[5,1000]{1,0:T(8,128)S(1)}, u32[]{:S(2)}, u32[]{:S(2)}) %collective-permute-start.1) | collective-permute-done | bytes 20032 | tf_op jit(solution)/shard_map/ppermute | solution.py:588
  60.9 0.1 reshape.21.index_ref.source_ref
  60.9 9.3 %shard_map.111 = (bf16[2016,256]{1,0:T(8,128)(2,1)S(1)}, bf16[2016,256]{1,0:T(8,128)(2,1)S(1)}) custom-call(s32[4000]{0:T(1024)S(1)} %reshape.21.index_ref.source_ref, f32[16384,128]{1,0:T(8,128)} %get-tuple-element.40.table_hbm.refs_5_), custom_call_target="tpu_custom_call" | custom-call | bytes 30000000 | tf_op jit(solution)/shard_map/pallas_call | solution.py:173
  70.2 0.5 slice.52
  70.7 1.0 copy-done.2
  71.7 1.2 copy-done.3
  73.0 6.4 %batch_terms.4 = (bf16[2016,256]{1,0:T(8,128)(2,1)}, f32[4032,128]{1,0:T(8,128)S(1)}, f32[64,256]{1,0:T(8,128)S(1)}) custom-call(s32[1]{0:T(128)} %bitcast.6.live_ref, s32[2,1024]{1,0:T(2,128)S(1)} %get-tuple-element.81.kind_ref, bf16[2016,256]{1,0:T(8,128)(2,1)S(1)} %copy-done.3, bf16[2016,256]{1,0:T(8,128)(2,1)S(1)} %get-tuple-element.41.target_ref, ...), custom_call_target="tpu_custom_call" | custom-call | bytes 15000000 | tf_op jit(solution)/shard_map/batch_terms/pallas_call | solution.py:271
  79.4 0.8 collective-permute-start.4
  80.2 1.6 batch_terms.5
  81.7 1.3 copy-done
  83.1 2.7 collective-permute-start.5
  85.9 0.6 fusion.3
  86.5 20.4 %collective-permute-done.4.refs_2_ = bf16[2016,256]{1,0:T(8,128)(2,1)} collective-permute-done((bf16[2016,256]{1,0:T(8,128)(2,1)}, bf16[2016,256]{1,0:T(8,128)(2,1)}, u32[]{:S(2)}, u32[]{:S(2)}) %collective-permute-start.4) | collective-permute-done | bytes 1032224 | tf_op jit(solution)/shard_map/ppermute | solution.py:588
  106.9 1.6 copy-done.1
  108.5 15.1 %first_total.2.refs_3_ = f32[16384,128]{1,0:T(8,128)} custom-call(s32[1]{0:T(128)} %bitcast.6.live_ref, s32[1]{0:T(128)} %bitcast.5.other_ref.refs_0_, s32[4000]{0:T(1024)S(1)} %reshape.21.index_ref.source_ref, s32[4000]{0:T(1024)S(1)} %copy-done.7, f32[4032,128]{1,0:T(8,128)S(1)} %get-tuple-element.42.refs_0_, f32[4032,128]{1,0:T(8,128)S(1)} %copy-done.1, ...), custom_call_target="tpu_custom_call" | custom-call | bytes 60000000 | tf_op jit(solution)/shard_map/first_total/pallas_call | solution.py:334
  123.5 1.2 collective-permute-done.5.refs_4_
  124.7 14.7 %finish_next.1 = (f32[16384,128]{1,0:T(8,128)}, f32[64,128]{1,0:T(8,128)S(1)}, bf16[2016,256]{1,0:T(8,128)(2,1)}) custom-call(s32[1]{0:T(128)} %bitcast.5.other_ref.refs_0_, s32[4000]{0:T(1024)S(1)} %copy-done.7, s32[4000]{0:T(1024)S(1)} %reshape_squeeze.13.refs_2_.index_ref.refs_1_, f32[16384,128]{1,0:T(8,128)} %first_total.2.refs_3_, ...), custom_call_target="tpu_custom_call" | custom-call | bytes 50000000 | tf_op jit(solution)/shard_map/finish_next/pallas_call | solution.py:432
  139.5 5.7 %collective-permute-start.6 = (bf16[2016,256]{1,0:T(8,128)(2,1)}, bf16[2016,256]{1,0:T(8,128)(2,1)S(1)}, u32[]{:S(2)}, u32[]{:S(2)}) collective-permute-start(bf16[2016,256]{1,0:T(8,128)(2,1)} %get-tuple-element.48), channel_id=1, source_target_pairs={{0,32},{4,36},{8,40},{12,44},{16,48},{20,52},{24,56},{28,60},{32,0... | collective-permute-start | bytes 3096584 | tf_op jit(solution)/shard_map/ppermute | solution.py:588
  145.1 8.0 %shard_map.115 = bf16[2016,256]{1,0:T(8,128)(2,1)} custom-call(s32[4000]{0:T(1024)} %copy-done.5, f32[16384,128]{1,0:T(8,128)} %get-tuple-element.50.table_hbm.refs_4_), custom_call_target="tpu_custom_call" | custom-call | bytes 30000000 | tf_op jit(solution)/shard_map/pallas_call | solution.py:173
  153.1 0.1 collective-permute-start.10
  153.3 2.0 collective-permute-start
  155.3 32.1 %collective-permute-done = s32[5,1000]{1,0:T(8,128)S(1)} collective-permute-done((s32[5,1000]{1,0:T(8,128)S(1)}, s32[5,1000]{1,0:T(8,128)S(1)}, u32[]{:S(2)}, u32[]{:S(2)}) %collective-permute-start) | collective-permute-done | bytes 20032 | tf_op jit(solution)/shard_map/ppermute | solution.py:588
  187.4 0.1 reshape.20.index_ref.source_ref
  187.5 0.5 slice.50
  188.0 1.7 collective-permute-start.7
  189.7 4.8 %collective-permute-start.8 = (f32[64,256]{1,0:T(8,128)S(1)}, f32[64,256]{1,0:T(8,128)S(1)}, u32[]{:S(2)}, u32[]{:S(2)}) collective-permute-start(f32[64,256]{1,0:T(8,128)S(1)} %get-tuple-element.54.refs_0_), channel_id=1, source_target_pairs={{0,64},{4,68},{8,72},{12,76},{16,80},{20,84},{24,88},{28,92},{32,9... | collective-permute-start | bytes 196616 | tf_op jit(solution)/shard_map/ppermute | solution.py:588
  194.6 9.3 %shard_map.113 = (bf16[2016,256]{1,0:T(8,128)(2,1)S(1)}, bf16[2016,256]{1,0:T(8,128)(2,1)S(1)}) custom-call(s32[4000]{0:T(1024)S(1)} %reshape.20.index_ref.source_ref, f32[16384,128]{1,0:T(8,128)} %get-tuple-element.50.table_hbm.refs_4_), custom_call_target="tpu_custom_call" | custom-call | bytes 30000000 | tf_op jit(solution)/shard_map/pallas_call | solution.py:173
  203.9 15.9 %shard_map.114 = (f32[64,256]{1,0:T(8,128)S(1)}, f32[64,256]{1,0:T(8,128)S(1)}) custom-call(f32[64,256]{1,0:T(8,128)S(1)} %get-tuple-element.54.refs_0_, f32[64,256]{1,0:T(8,128)S(1)} %collective-permute-done.7.refs_1_, f32[64,256]{1,0:T(8,128)S(1)} %collective-permute-done.8.refs_2_, f32[64,256]{1,0:T(8,128)S(1)} %collective-permute-done.9.refs_3_, ...), custom_call_target="tpu_custom_call" | custom-call | bytes 20000000 | tf_op jit(solution)/shard_map/pallas_call | solution.py:537
  219.8 5.4 %batch_terms.6 = (bf16[2016,256]{1,0:T(8,128)(2,1)S(1)}, f32[4032,128]{1,0:T(8,128)S(1)}, f32[64,256]{1,0:T(8,128)S(1)}) custom-call(s32[1]{0:T(128)} %bitcast.4.live_ref, s32[2,1024]{1,0:T(2,128)S(1)} %get-tuple-element.79.kind_ref, bf16[2016,256]{1,0:T(8,128)(2,1)S(1)} %collective-permute-done.6.source_ref, ...), custom_call_target="tpu_custom_call" | custom-call | bytes 15000000 | tf_op jit(solution)/shard_map/batch_terms/pallas_call | solution.py:271
  225.3 0.1 collective-permute-start.11
  225.4 5.6 %batch_terms.7 = (bf16[2016,256]{1,0:T(8,128)(2,1)S(1)}, f32[4032,128]{1,0:T(8,128)S(1)}, f32[64,256]{1,0:T(8,128)S(1)}) custom-call(s32[1]{0:T(128)} %bitcast.4.live_ref, s32[2,1024]{1,0:T(2,128)S(1)} %get-tuple-element.78.kind_ref, bf16[2016,256]{1,0:T(8,128)(2,1)S(1)} %collective-permute-done.10.source_ref, ...), custom_call_target="tpu_custom_call" | custom-call | bytes 15000000 | tf_op jit(solution)/shard_map/batch_terms/pallas_call | solution.py:271
  231.0 0.1 collective-permute-start.12
  231.1 15.5 %shard_map.116 = f32[64,256]{1,0:T(8,128)S(1)} custom-call(f32[64,256]{1,0:T(8,128)S(1)} %get-tuple-element.68.own), custom_call_target="tpu_custom_call" | custom-call | bytes 20000000 | tf_op jit(solution)/shard_map/pallas_call | solution.py:537
  246.6 0.2 collective-permute-start.13
  246.8 2.5 collective-permute-start.14
  249.3 2.1 collective-permute-start.15
  251.4 23.2 %collective-permute-done.13 = f32[64,256]{1,0:T(8,128)S(1)} collective-permute-done((f32[64,256]{1,0:T(8,128)S(1)}, f32[64,256]{1,0:T(8,128)S(1)}, u32[]{:S(2)}, u32[]{:S(2)}) %collective-permute-start.13) | collective-permute-done | bytes 65568 | tf_op jit(solution)/shard_map/ppermute | solution.py:588
  274.6 1.0 collective-permute-done.14
  275.6 0.7 multiply_subtract_fusion
  276.2 20.8 %first_total.3.refs_2_ = f32[16384,128]{1,0:T(8,128)} custom-call(s32[1]{0:T(128)} %bitcast.4.live_ref, s32[1]{0:T(128)} %bitcast.other_ref.refs_0_, s32[4000]{0:T(1024)S(1)} %reshape.20.index_ref.source_ref, s32[4000]{0:T(1024)S(1)} %copy-done.6, f32[4032,128]{1,0:T(8,128)S(1)} %get-tuple-element.59.refs_0_, f32[4032,128]{1,0:T(8,128)S(1)} %get-tuple-element.62.refs_1_, ...), custom_call_target="tpu_custom_call" | custom-call | bytes 60000000 | tf_op jit(solution)/shard_map/first_total/pallas_call | solution.py:334
  297.1 12.5 %finish_last.1 = (f32[8192,256]{1,0:T(8,128)}, f32[64,128]{1,0:T(8,128)}) custom-call(s32[1]{0:T(128)} %bitcast.other_ref.refs_0_, s32[4000]{0:T(1024)S(1)} %copy-done.6, f32[16384,128]{1,0:T(8,128)} %first_total.3.refs_2_, bf16[2016,256]{1,0:T(8,128)(2,1)S(1)} %collective-permute-done.12.refs_3_, f32[16384,128]{1,0:T(8,128)} %get-tuple-element.50.table_hbm.refs_4_, ...), custom_call_target="tpu_custom_call" | custom-call | bytes 50000000 | tf_op jit(solution)/shard_map/finish_last/pallas_call | solution.py:432
  (41 shorter events, 0.3 us)
Async XLA Ops:
  11.0 12.1 %copy-start.12 = (s32[5,1000]{1,0:T(8,128)S(1)}, s32[5,1000]{1,0:T(8,128)}, u32[]{:S(2)}) copy-start(s32[5,1000]{1,0:T(8,128)} %get-tuple-element.38) | copy-start | bytes 60004
  11.0 59.7 %collective-permute-start.2 = (bf16[2016,256]{1,0:T(8,128)(2,1)}, bf16[2016,256]{1,0:T(8,128)(2,1)S(1)}, u32[]{:S(2)}, u32[]{:S(2)}) collective-permute-start(bf16[2016,256]{1,0:T(8,128)(2,1)} %get-tuple-element.39), channel_id=1, source_target_pairs={{0,64},{4,68},{8,72},{12,76},{16,80},{20,84},{24,88},{28,92},{32,9... | collective-permute-start | bytes 3096584 | tf_op jit(solution)/shard_map/ppermute | solution.py:588
  15.0 56.8 %copy-start.4 = (f32[64,256]{1,0:T(8,128)S(1)}, f32[64,256]{1,0:T(8,128)}, u32[]{:S(2)}) copy-start(f32[64,256]{1,0:T(8,128)} %refs_4_.1) | copy-start | bytes 196612
  23.0 62.9 %copy-start.10 = (s32[1,1,2]{2,1,0:T(1,128)S(1)}, s32[1,1,2]{2,1,0:T(1,128)}, u32[]{:S(2)}) copy-start(s32[1,1,2]{2,1,0:T(1,128)} %param.15) | copy-start | bytes 28
  23.0 83.9 %copy-start.7 = (s32[4000]{0:T(1024)S(1)}, s32[4000]{0:T(1024)}, u32[]{:S(2)}) copy-start(s32[4000]{0:T(1024)} %reshape_squeeze.14.index_ref.refs_1_) | copy-start | bytes 48004
  23.0 57.1 %collective-permute-start.3 = (bf16[2016,256]{1,0:T(8,128)(2,1)}, bf16[2016,256]{1,0:T(8,128)(2,1)S(1)}, u32[]{:S(2)}, u32[]{:S(2)}) collective-permute-start(bf16[2016,256]{1,0:T(8,128)(2,1)} %shard_map.112), channel_id=1, source_target_pairs={{0,64},{4,68},{8,72},{12,76},{16,80},{20,84},{24,88},{28,92},{32,9... | collective-permute-start | bytes 3096584 | tf_op jit(solution)/shard_map/ppermute | solution.py:588
  23.1 37.7 %collective-permute-start.1 = (s32[5,1000]{1,0:T(8,128)S(1)}, s32[5,1000]{1,0:T(8,128)S(1)}, u32[]{:S(2)}, u32[]{:S(2)}) collective-permute-start(s32[5,1000]{1,0:T(8,128)S(1)} %copy-done.12), channel_id=1, source_target_pairs={{0,64},{4,68},{8,72},{12,76},{16,80},{20,84},{24,88},{28,92},{32,9... | collective-permute-start | bytes 60008 | tf_op jit(solution)/shard_map/ppermute | solution.py:588
  70.7 1.0 copy-start.2
  71.7 1.2 copy-start.3
  79.4 45.3 %copy-start.9 = (f32[8192]{0:T(1024)S(1)}, f32[8192]{0:T(1024)}, u32[]{:S(2)}) copy-start(f32[8192]{0:T(1024)} %param.9) | copy-start | bytes 98308
  79.4 27.5 %collective-permute-start.4 = (bf16[2016,256]{1,0:T(8,128)(2,1)}, bf16[2016,256]{1,0:T(8,128)(2,1)}, u32[]{:S(2)}, u32[]{:S(2)}) collective-permute-start(bf16[2016,256]{1,0:T(8,128)(2,1)} %get-tuple-element.46), channel_id=1, source_target_pairs={{0,64},{4,68},{8,72},{12,76},{16,80},{20,84},{24,88},{28,92},{32,9... | collective-permute-start | bytes 3096584 | tf_op jit(solution)/shard_map/ppermute | solution.py:588
  81.7 1.4 copy-start
  83.1 41.7 %collective-permute-start.5 = (bf16[2016,256]{1,0:T(8,128)(2,1)}, bf16[2016,256]{1,0:T(8,128)(2,1)S(1)}, u32[]{:S(2)}, u32[]{:S(2)}) collective-permute-start(bf16[2016,256]{1,0:T(8,128)(2,1)} %get-tuple-element.47), channel_id=1, source_target_pairs={{0,64},{4,68},{8,72},{12,76},{16,80},{20,84},{24,88},{28,92},{32,9... | collective-permute-start | bytes 3096584 | tf_op jit(solution)/shard_map/ppermute | solution.py:588
  85.9 53.6 %copy-start.5 = (s32[4000]{0:T(1024)}, s32[4000]{0:T(1024)S(1)}, u32[]{:S(2)}) copy-start(s32[4000]{0:T(1024)S(1)} %reshape_squeeze.13.refs_2_.index_ref.refs_1_) | copy-start | bytes 48004
  106.9 1.6 copy-start.1
  139.5 13.8 %copy-start.11 = (s32[5,1000]{1,0:T(8,128)S(1)}, s32[5,1000]{1,0:T(8,128)}, u32[]{:S(2)}) copy-start(s32[5,1000]{1,0:T(8,128)} %get-tuple-element.37) | copy-start | bytes 60004
  139.5 80.3 %collective-permute-start.6 = (bf16[2016,256]{1,0:T(8,128)(2,1)}, bf16[2016,256]{1,0:T(8,128)(2,1)S(1)}, u32[]{:S(2)}, u32[]{:S(2)}) collective-permute-start(bf16[2016,256]{1,0:T(8,128)(2,1)} %get-tuple-element.48), channel_id=1, source_target_pairs={{0,32},{4,36},{8,40},{12,44},{16,48},{20,52},{24,56},{28,60},{32,0... | collective-permute-start | bytes 3096584 | tf_op jit(solution)/shard_map/ppermute | solution.py:588
  145.1 58.7 %copy-start.8 = (f32[64,256]{1,0:T(8,128)S(1)}, f32[64,256]{1,0:T(8,128)}, u32[]{:S(2)}) copy-start(f32[64,256]{1,0:T(8,128)} %refs_5_.1) | copy-start | bytes 196612
  153.1 123.1 %copy-start.6 = (s32[4000]{0:T(1024)S(1)}, s32[4000]{0:T(1024)}, u32[]{:S(2)}) copy-start(s32[4000]{0:T(1024)} %copy-done.5) | copy-start | bytes 48004
  153.1 72.2 %collective-permute-start.10 = (bf16[2016,256]{1,0:T(8,128)(2,1)}, bf16[2016,256]{1,0:T(8,128)(2,1)S(1)}, u32[]{:S(2)}, u32[]{:S(2)}) collective-permute-start(bf16[2016,256]{1,0:T(8,128)(2,1)} %shard_map.115), channel_id=1, source_target_pairs={{0,32},{4,36},{8,40},{12,44},{16,48},{20,52},{24,56},{28,60},{32,0... | collective-permute-start | bytes 3096584 | tf_op jit(solution)/shard_map/ppermute | solution.py:588
  153.3 34.1 %collective-permute-start = (s32[5,1000]{1,0:T(8,128)S(1)}, s32[5,1000]{1,0:T(8,128)S(1)}, u32[]{:S(2)}, u32[]{:S(2)}) collective-permute-start(s32[5,1000]{1,0:T(8,128)S(1)} %copy-done.11), channel_id=1, source_target_pairs={{0,32},{4,36},{8,40},{12,44},{16,48},{20,52},{24,56},{28,60},{32,0... | collective-permute-start | bytes 60008 | tf_op jit(solution)/shard_map/ppermute | solution.py:588
  188.0 15.9 %collective-permute-start.7 = (f32[64,256]{1,0:T(8,128)S(1)}, f32[64,256]{1,0:T(8,128)S(1)}, u32[]{:S(2)}, u32[]{:S(2)}) collective-permute-start(f32[64,256]{1,0:T(8,128)S(1)} %get-tuple-element.54.refs_0_), channel_id=1, source_target_pairs={{0,32},{4,36},{8,40},{12,44},{16,48},{20,52},{24,56},{28,60},{32,0... | collective-permute-start | bytes 196616 | tf_op jit(solution)/shard_map/ppermute | solution.py:588
  189.7 14.1 %collective-permute-start.8 = (f32[64,256]{1,0:T(8,128)S(1)}, f32[64,256]{1,0:T(8,128)S(1)}, u32[]{:S(2)}, u32[]{:S(2)}) collective-permute-start(f32[64,256]{1,0:T(8,128)S(1)} %get-tuple-element.54.refs_0_), channel_id=1, source_target_pairs={{0,64},{4,68},{8,72},{12,76},{16,80},{20,84},{24,88},{28,92},{32,9... | collective-permute-start | bytes 196616 | tf_op jit(solution)/shard_map/ppermute | solution.py:588
  194.5 9.3 %collective-permute-start.9 = (f32[64,256]{1,0:T(8,128)S(1)}, f32[64,256]{1,0:T(8,128)S(1)}, u32[]{:S(2)}, u32[]{:S(2)}) collective-permute-start(f32[64,256]{1,0:T(8,128)S(1)} %get-tuple-element.54.refs_0_), channel_id=1, source_target_pairs={{0,96},{4,100},{8,104},{12,108},{16,112},{20,116},{24,120},{28,124... | collective-permute-start | bytes 196616 | tf_op jit(solution)/shard_map/ppermute | solution.py:588
  225.3 51.0 %collective-permute-start.11 = (bf16[2016,256]{1,0:T(8,128)(2,1)S(1)}, bf16[2016,256]{1,0:T(8,128)(2,1)S(1)}, u32[]{:S(2)}, u32[]{:S(2)}) collective-permute-start(bf16[2016,256]{1,0:T(8,128)(2,1)S(1)} %get-tuple-element.63), channel_id=1, source_target_pairs={{0,32},{4,36},{8,40},{12,44},{16,48},{20,52},{24,56},{28,60},{32,0... | collective-permute-start | bytes 3096584 | tf_op jit(solution)/shard_map/ppermute | solution.py:588
  231.0 66.1 %collective-permute-start.12 = (bf16[2016,256]{1,0:T(8,128)(2,1)S(1)}, bf16[2016,256]{1,0:T(8,128)(2,1)S(1)}, u32[]{:S(2)}, u32[]{:S(2)}) collective-permute-start(bf16[2016,256]{1,0:T(8,128)(2,1)S(1)} %get-tuple-element.64), channel_id=1, source_target_pairs={{0,32},{4,36},{8,40},{12,44},{16,48},{20,52},{24,56},{28,60},{32,0... | collective-permute-start | bytes 3096584 | tf_op jit(solution)/shard_map/ppermute | solution.py:588
  246.6 27.9 %collective-permute-start.13 = (f32[64,256]{1,0:T(8,128)S(1)}, f32[64,256]{1,0:T(8,128)S(1)}, u32[]{:S(2)}, u32[]{:S(2)}) collective-permute-start(f32[64,256]{1,0:T(8,128)S(1)} %shard_map.116), channel_id=1, source_target_pairs={{0,32},{4,36},{8,40},{12,44},{16,48},{20,52},{24,56},{28,60},{32,0... | collective-permute-start | bytes 196616 | tf_op jit(solution)/shard_map/ppermute | solution.py:588
  246.8 28.7 %collective-permute-start.14 = (f32[64,256]{1,0:T(8,128)S(1)}, f32[64,256]{1,0:T(8,128)S(1)}, u32[]{:S(2)}, u32[]{:S(2)}) collective-permute-start(f32[64,256]{1,0:T(8,128)S(1)} %shard_map.116), channel_id=1, source_target_pairs={{0,64},{4,68},{8,72},{12,76},{16,80},{20,84},{24,88},{28,92},{32,9... | collective-permute-start | bytes 196616 | tf_op jit(solution)/shard_map/ppermute | solution.py:588
  249.3 26.2 %collective-permute-start.15 = (f32[64,256]{1,0:T(8,128)S(1)}, f32[64,256]{1,0:T(8,128)S(1)}, u32[]{:S(2)}, u32[]{:S(2)}) collective-permute-start(f32[64,256]{1,0:T(8,128)S(1)} %shard_map.116), channel_id=1, source_target_pairs={{0,96},{4,100},{8,104},{12,108},{16,112},{20,116},{24,120},{28,124... | collective-permute-start | bytes 196616 | tf_op jit(solution)/shard_map/ppermute | solution.py:588
